TPU v7x, 1024 devices: a whole 4x8x16 slice. The times are simulated.
1024 devices in a mesh: ctx: 16 (over y, core), dp: 16 (over z), pipe: 4 (over x).
Axes of the slice: x: 4, y: 8, z: 16, core: 2. Of those that a mesh axis runs over, the one named last changes fastest.
Arguments:
- queries: bfloat16 [1, 16384, 8192], P(None, 'ctx', ('dp', 'pipe')), may hold values from -2 to 2
- key_tokens: bfloat16 [1, 16384, 8192], P(None, 'ctx', ('dp', 'pipe')), may hold values from -2 to 2
- values: bfloat16 [1, 16384, 8192], P(None, 'ctx', ('dp', 'pipe')), may hold values from -6 to 6
- gate_logits: bfloat16 [1, 16384, 8192], P(None, 'ctx', ('dp', 'pipe')), may hold values from -6 to 6
- cotangent: bfloat16 [1, 16384, 8192], P(None, 'ctx', ('dp', 'pipe')), may hold values from -6 to 6
- decay_rates: float32 [64], P(('dp', 'pipe')), may hold values from 3.0517578e-05 to 0.05
- norm_gain: float32 [64, 128], P(('dp', 'pipe')), may hold values from 0.5 to 1.5
- block_starts: int32 [1, 64], P(None, 'ctx'), may hold values 0 or 1
Outputs:
- mixed_out: bfloat16 [1, 16384, 8192], P(None, 'ctx', ('dp', 'pipe'))
- query_grad: bfloat16 [1, 16384, 8192], P(None, 'ctx', ('dp', 'pipe'))
- key_grad: bfloat16 [1, 16384, 8192], P(None, 'ctx', ('dp', 'pipe'))
- value_grad: bfloat16 [1, 16384, 8192], P(None, 'ctx', ('dp', 'pipe'))
- gate_grad: bfloat16 [1, 16384, 8192], P(None, 'ctx', ('dp', 'pipe'))
- gain_grad: float32 [64, 128], P(('dp', 'pipe'))
All inputs are finite; a program needn't handle non-finite values. No bound on the sum of `block_starts` on one device may be relied on, other than what follows from the above.
Results may differ from a plain program's by a relative error of at most 0.0012.
Values sent between devices are 32-bit elements; how exact they have to be, the bound alone decides.
No kernel may reach another device: no remote copies, remote signals or barrier semaphores. Data moves between devices by JAX's collectives and lax.ppermute only.
A program may use at most 32 MiB of HBM per device.

v0:
```python
import math

import jax
import jax.numpy as jnp
from jax import lax
from jax.sharding import PartitionSpec as P

BLOCK = 256


highest = lax.Precision.HIGHEST
epsilon = 1e-06


def sent_to_all(shard, axis):
    peers = lax.axis_size(axis)
    return lax.all_to_all(
        jnp.broadcast_to(shard[None], (peers, *shard.shape)), axis, 0, 0, tiled=True
    )


def gathered_once(shard, axis):
    leaves = jax.tree.leaves(shard)
    turns = sorted(range(len(leaves)), key=lambda k: -leaves[k].size)
    width = (1, *leaves[turns[0]].shape)[-1]
    lines = [
        jnp.pad(leaves[k].reshape(-1), (0, -leaves[k].size % width)).reshape(-1, width)
        for k in turns
    ]
    both, at, found = (sent_to_all(jnp.concatenate(lines), axis), 0, {})
    for k, line in zip(turns, lines):
        slab = both[:, at : at + len(line)].reshape(len(both), -1)
        found[k] = slab[:, : leaves[k].size].reshape(-1, *leaves[k].shape)
        at += len(line)
    numbers = iter(range(len(leaves)))
    return jax.tree.map(lambda _: found[next(numbers)], shard)


def folded_in_pairs(pieces, combine):
    while len(jax.tree.leaves(pieces)[0]) > 1:
        pieces = jax.vmap(combine)(
            *(jax.tree.map(lambda part: part[side::2], pieces) for side in (0, 1))
        )
    return jax.tree.map(lambda part: part[0], pieces)


def prefix(shard, axis, combine, identity, reverse):
    peers, index = (lax.axis_size(axis), lax.axis_index(axis))
    passed = jnp.arange(peers) > index if reverse else jnp.arange(peers) < index

    def kept(part, zero, own):
        part = jnp.where(
            passed.reshape(-1, *(1 for _ in own.shape)), part, jnp.asarray(zero, own.dtype)
        )
        return part[::-1] if reverse else part

    pieces = gathered_once(shard, axis)
    return folded_in_pairs(jax.tree.map(kept, pieces, identity, shard), combine)


def of_everyone(shard, axis):
    return sent_to_all(shard, axis).sum(axis=0)


def packed_total(arrays, axis):
    ends = [0]
    for a in arrays:
        ends.append(ends[-1] + a.size)
    subtotal = of_everyone(jnp.concatenate([a.ravel() for a in arrays]), axis)
    return tuple((subtotal[b:e].reshape(a.shape) for a, b, e in zip(arrays, ends, ends[1:])))


def run_blocks(query_rows, key_rows, value_rows, decay_rate, block_flags, block_size):
    block_count = query_rows.shape[0] // block_size
    query_blocks = query_rows.reshape(block_count, block_size, -1)
    key_blocks = key_rows.reshape(block_count, block_size, -1)
    value_blocks = value_rows.reshape(block_count, block_size, -1)
    offsets = jnp.arange(block_size, dtype=jnp.float32)
    distance = offsets[:, None] - offsets[None, :]
    weights = jnp.where(distance >= 0, jnp.exp(-decay_rate * jnp.maximum(distance, 0.0)), 0.0)
    decay_in = jnp.exp(-decay_rate * offsets)
    decay_out = jnp.exp(-decay_rate * (block_size - offsets))
    decay_block = jnp.exp(-decay_rate * block_size)

    def advance(carried, pieces):
        query_part, key_part, value_part, flag = pieces
        carried = carried * (1.0 - flag)
        scores = jnp.dot(query_part, key_part.T, precision=highest) * weights
        result = jnp.dot(scores, value_part, precision=highest) + decay_in[:, None] * jnp.dot(
            query_part, carried, precision=highest
        )
        carried = decay_block * carried + jnp.dot(
            key_part.T, decay_out[:, None] * value_part, precision=highest
        )
        return (carried, result)

    initial = jnp.zeros((key_rows.shape[1], value_rows.shape[1]), jnp.float32)
    closing, results = lax.scan(
        advance, initial, (query_blocks, key_blocks, value_blocks, block_flags)
    )
    return (results.reshape(query_rows.shape[0], -1), closing)


def to_heads(array, head_count):
    token_count = array.shape[1]
    return array[0].astype(jnp.float32).reshape(token_count, head_count, -1).transpose(1, 0, 2)


def from_heads(array):
    return array.transpose(1, 0, 2).reshape(1, array.shape[1], -1)


def flipped(array):
    return jnp.flip(array, axis=1)


def compose(earlier, later):
    return (later[0] * earlier[0], later[0][:, None, None] * earlier[1] + later[1])


def body(queries, key_tokens, values, gate_logits, cotangent, decay_rates, norm_gain, block_starts):
    head_count = decay_rates.shape[0]
    token_count = queries.shape[1]
    start_flags = block_starts[0].astype(jnp.float32)
    reverse_flags = jnp.flip(jnp.concatenate([start_flags[1:], jnp.zeros((1,), jnp.float32)]))

    def forward_run(query_rows, key_rows, value_rows, decay_rate):
        return run_blocks(query_rows, key_rows, value_rows, decay_rate, start_flags, BLOCK)

    def backward_run(query_rows, key_rows, value_rows, decay_rate):
        return run_blocks(query_rows, key_rows, value_rows, decay_rate, reverse_flags, BLOCK)

    forward_many = jax.vmap(forward_run)
    backward_many = jax.vmap(backward_run)
    query_heads = to_heads(queries, head_count)
    key_heads = to_heads(key_tokens, head_count)
    value_heads = to_heads(values, head_count)
    local_out, closing = forward_many(query_heads, key_heads, value_heads, decay_rates)
    unbroken = jnp.prod(1.0 - start_flags)
    carry_rate = jnp.exp(-decay_rates * token_count) * unbroken
    identity = (jnp.ones_like(carry_rate), jnp.zeros_like(closing))
    state_in = prefix((carry_rate, closing), "ctx", compose, identity, False)[1]
    positions = jnp.arange(token_count, dtype=jnp.float32)
    open_head = (jnp.cumsum(start_flags) == 0).astype(jnp.float32)
    weight_in = (
        jnp.exp(-decay_rates[:, None] * positions[None, :]) * jnp.repeat(open_head, BLOCK)[None, :]
    )
    attended = local_out + weight_in[:, :, None] * jnp.einsum(
        "hld,hde->hle", query_heads, state_in, precision=highest
    )
    mixed = from_heads(attended)[0]
    gain_flat = norm_gain.reshape(-1)
    gate_open = jax.nn.sigmoid(gate_logits[0].astype(jnp.float32))
    grad_out = cotangent[0].astype(jnp.float32)
    grad_norm = grad_out * gate_open * gain_flat
    local_sq = jnp.sum(mixed * mixed, axis=1)
    local_cross = jnp.sum(grad_norm * mixed, axis=1)
    inner_sq, inner_cross = (of_everyone(local_sq, "pipe"), of_everyone(local_cross, "pipe"))
    sq_sum, cross_dot = packed_total((inner_sq, inner_cross), "dp")
    feature_total = mixed.shape[1] * lax.axis_size("dp") * lax.axis_size("pipe")
    inverse = lax.rsqrt(sq_sum / feature_total + epsilon)
    normed = mixed * inverse[:, None]
    mixed_out = (gate_open * gain_flat * normed).astype(jnp.bfloat16)[None]
    gate_grad = (grad_out * gain_flat * normed * gate_open * (1.0 - gate_open)).astype(
        jnp.bfloat16
    )[None]
    grad_mixed = inverse[:, None] * (
        grad_norm - normed * (inverse * cross_dot / feature_total)[:, None]
    )
    grad_heads = to_heads(grad_mixed[None], head_count)
    query_local, unused = forward_many(grad_heads, value_heads, key_heads, decay_rates)
    query_total = query_local + weight_in[:, :, None] * jnp.einsum(
        "hle,hde->hld", grad_heads, state_in, precision=highest
    )
    query_grad = from_heads(query_total).astype(jnp.bfloat16)
    back_keys = flipped(key_heads)
    back_values = flipped(value_heads)
    value_local, value_closing = backward_many(
        back_keys, flipped(query_heads), flipped(grad_heads), decay_rates
    )
    key_local, key_closing = backward_many(
        back_values, flipped(grad_heads), flipped(query_heads), decay_rates
    )
    kept_tail = 1.0 - start_flags[0]
    open_tail = (jnp.cumsum(reverse_flags) == 0).astype(jnp.float32)
    weight_back = (
        jnp.exp(-decay_rates[:, None] * positions[None, :]) * jnp.repeat(open_tail, BLOCK)[None, :]
    )
    value_state = prefix((carry_rate, value_closing * kept_tail), "ctx", compose, identity, True)[1]
    key_state = jnp.swapaxes(value_state, 1, 2)
    value_total = value_local + weight_back[:, :, None] * jnp.einsum(
        "hld,hde->hle", back_keys, value_state, precision=highest
    )
    key_total = key_local + weight_back[:, :, None] * jnp.einsum(
        "hld,hde->hle", back_values, key_state, precision=highest
    )
    value_grad = from_heads(flipped(value_total)).astype(jnp.bfloat16)
    key_grad = from_heads(flipped(key_total)).astype(jnp.bfloat16)
    row_total = token_count * lax.axis_size("ctx")
    gain_part = (jnp.sum(grad_out * gate_open * normed, axis=0) / math.sqrt(row_total)).reshape(
        head_count, -1
    )
    gain_grad = of_everyone(gain_part, "ctx")
    return (mixed_out, query_grad, key_grad, value_grad, gate_grad, gain_grad)


def solution(mesh):
    placed = (
        P(None, "ctx", ("dp", "pipe")),
        P(None, "ctx", ("dp", "pipe")),
        P(None, "ctx", ("dp", "pipe")),
        P(None, "ctx", ("dp", "pipe")),
        P(None, "ctx", ("dp", "pipe")),
        P(("dp", "pipe")),
        P(("dp", "pipe"), None),
        P(None, "ctx"),
    )
    return jax.shard_map(
        body,
        mesh=mesh,
        in_specs=placed,
        out_specs=(
            P(None, "ctx", ("dp", "pipe")),
            P(None, "ctx", ("dp", "pipe")),
            P(None, "ctx", ("dp", "pipe")),
            P(None, "ctx", ("dp", "pipe")),
            P(None, "ctx", ("dp", "pipe")),
            P(("dp", "pipe"), None),
        ),
        check_vma=False,
    )
```

profile of v0, /device:TPU:1, one launch (start us, length us, event | category | flops | bytes accessed | tf_op | source)
XLA Modules:
  0.0 212.7 jit_solution(2938749742717848242)
XLA Ops:
  1.4 1.3 subtract_reduce_fusion
  5.4 11.2 %while.60 = (s32[]{:T(128)}, f32[1,128,128]{2,1,0:T(8,128)S(1)}, f32[4,1,256,128]{3,2,1,0:T(8,128)S(1)}, f32[1]{0:T(128)}, f32[4]{0:T(128)S(1)}, /*index=5*/f32[...) while((s32[]{:T(128)}, f32[1,128,128]{2,1,0:T(8,128)S(1)}, ...), condition=%wide.region_1.2_spmd.clone.clone.clone, body=%wide.region_0.1_spmd.clone.clone.clone.sunk | while | flops 302580480 | bytes 1908407 | solution.py:98
  17.4 1.1 broadcast_in_dim.66
  18.4 17.7 %all-to-all-start = ((f32[16,129,128]{2,1,0:T(8,128)}), f32[16,129,128]{2,1,0:T(8,128)S(1)}, u32[]{:S(2)}, u32[]{:S(2)}) async-start(f32[16,129,128]{2,1,0:T(8,128)} %broadcast_in_dim.66), calls=%async_computation | async-start | bytes 2228224 | tf_op jit(solution)/shard_map/all_to_all | solution.py:17
  36.3 1.2 copy.83
  39.4 26.2 %all-to-all-done = f32[16,129,128]{2,1,0:T(8,128)S(1)} async-done(((f32[16,129,128]{2,1,0:T(8,128)}), f32[16,129,128]{2,1,0:T(8,128)S(1)}, u32[]{:S(2)}, u32[]{:S(2)}) %all-to-all-start) | async-done | bytes 1056800 | tf_op jit(solution)/shard_map/all_to_all | solution.py:17
  67.8 1.2 multiply_reduce_fusion.1
  69.1 6.6 %all_to_all.33 = f32[4,1,1024]{2,1,0:T(1,128)S(1)} all-to-all(f32[4,1,1024]{2,1,0:T(1,128)S(1)} %broadcast_in_dim.74), channel_id=1, replica_groups=mesh['ctx'=16,'dp'=16,'pipe'=4] {'pipe'}, dimensions={0} | all-to-all | bytes 32768 | tf_op jit(solution)/shard_map/all_to_all | solution.py:17
  76.3 3.3 %all-to-all-start.1 = ((f32[4,1,1024]{2,1,0:T(1,128)}), f32[4,1,1024]{2,1,0:T(1,128)S(1)}, u32[]{:S(2)}, u32[]{:S(2)}) async-start(f32[4,1,1024]{2,1,0:T(1,128)} %broadcast_in_dim.70), calls=%async_computation.1 | async-start | bytes 32768 | tf_op jit(solution)/shard_map/all_to_all | solution.py:17
  79.9 3.8 %all-to-all-done.1 = f32[4,1,1024]{2,1,0:T(1,128)S(1)} async-done(((f32[4,1,1024]{2,1,0:T(1,128)}), f32[4,1,1024]{2,1,0:T(1,128)S(1)}, u32[]{:S(2)}, u32[]{:S(2)}) %all-to-all-start.1) | async-done | bytes 16416 | tf_op jit(solution)/shard_map/all_to_all | solution.py:17
  84.5 11.0 %all-to-all-start.3 = ((f32[16,1,2048]{2,1,0:T(1,128)}), f32[16,1,2048]{2,1,0:T(1,128)S(1)}, u32[]{:S(2)}, u32[]{:S(2)}) async-start(f32[16,1,2048]{2,1,0:T(1,128)} %broadcast_in_dim.75), calls=%async_computation.3 | async-start | bytes 262144 | tf_op jit(solution)/shard_map/all_to_all | solution.py:17
  95.7 1.8 convert_bitcast_fusion.3
  97.5 3.4 %reverse.25 = f32[1024,128]{1,0:T(8,128)S(1)} reverse(f32[1024,128]{1,0:T(8,128)} %convert_bitcast_fusion.3), dimensions={0} | reverse | bytes 1048576 | tf_op jit(solution)/shard_map/reverse.3
  102.6 4.9 %all-to-all-done.3 = f32[16,1,2048]{2,1,0:T(1,128)S(1)} async-done(((f32[16,1,2048]{2,1,0:T(1,128)}), f32[16,1,2048]{2,1,0:T(1,128)S(1)}, u32[]{:S(2)}, u32[]{:S(2)}) %all-to-all-start.3) | async-done | bytes 131104 | tf_op jit(solution)/shard_map/all_to_all | solution.py:17
  107.6 2.2 %fusion.142 = (bf16[1,1024,128]{1,2,0:T(8,128)(2,1)}, bf16[1,1024,128]{1,2,0:T(8,128)(2,1)}, f32[1,1024,128]{1,2,0:T(8,128)}) fusion(bf16[1,1024,128]{1,2,0:T(8,128)(2,1)} %copy-done, f32[1024,128]{0,1:T(8,128)S(1)} %get-tuple-element.861, f32[1024]{0:T(1024)S(1)} %get-tuple-element.844, f32[128]{0:T(128)S(1)} %bitcast.439, bf16[1,1024,128]{1,2,0:T(8,128)(2,1)} %copy-done.2), kind=kLoop, calls=%fused_computation.174 | loop fusion | flops 2097152 | bytes 2101760 | tf_op jit(solution)/shard_map/convert_element_type | solution.py:164
  109.8 2.1 copy.102
  111.9 2.3 %subtract_multiply_fusion.1 = f32[4,1,256,128]{3,2,1,0:T(8,128)} fusion(f32[4,1,256,128]{3,2,1,0:T(8,128)} %bitcast.413, f32[4,1,256,128]{3,2,1,0:T(8,128)} %bitcast.415, f32[4,256]{1,0:T(4,128)S(1)} %multiply_multiply_fusion.1, f32[128]{0:T(128)S(1)} %bitcast.440, f32[4,256]{1,0:T(4,128)S(1)} %rsqrt.9), kind=kLoop, calls=%fused_computation.186 | loop fusion | flops 655360 | bytes 1581568 | tf_op jit(solution)/shard_map/mul | solution.py:167
  115.0 20.7 %while.61 = (s32[]{:T(128)}, f32[1,128,128]{2,1,0:T(8,128)S(1)}, f32[4,1,256,128]{3,2,1,0:T(8,128)}, f32[1]{0:T(128)}, f32[4]{0:T(128)S(1)}, /*index=5*/f32[4,1,...) while((s32[]{:T(128)}, f32[1,128,128]{2,1,0:T(8,128)S(1)}, ...), condition=%wide.region_10.11_spmd.clone.clone.clone, body=%wide.region_9.10_spmd.clone.clone.clone.sunk | while | flops 302580480 | bytes 1909423 | solution.py:98
  116.2 1.2 convolution_multiply_fusion.22
  117.8 1.3 convolution_multiply_fusion.23
  119.1 1.0 fusion.241
  121.3 1.2 convolution_multiply_fusion.22
  123.0 1.3 convolution_multiply_fusion.23
  124.3 1.1 fusion.241
  126.5 1.2 convolution_multiply_fusion.22
  128.2 1.3 convolution_multiply_fusion.23
  129.5 1.0 fusion.241
  131.7 1.2 convolution_multiply_fusion.22
  133.3 1.3 convolution_multiply_fusion.23
  134.6 1.1 fusion.241
  135.7 1.4 fusion.147
  138.8 13.7 %while.63 = (s32[]{:T(128)}, f32[1,128,128]{2,1,0:T(8,128)S(1)}, f32[4,1,256,128]{3,2,1,0:T(8,128)}, f32[1]{0:T(128)}, f32[4]{0:T(128)S(1)}, /*index=5*/f32[4,1,...) while((s32[]{:T(128)}, f32[1,128,128]{2,1,0:T(8,128)S(1)}, ...), condition=%wide.region_15.16_spmd.clone.clone.clone, body=%wide.region_14.15_spmd.clone.clone.clone.sunk | while | flops 302580480 | bytes 1908407 | solution.py:98
  148.1 1.1 fusion.261
  151.5 1.0 fusion.261
  153.2 7.7 %all-to-all-start.5 = ((f32[16,1,128]{2,1,0:T(1,128)}), f32[16,1,128]{2,1,0:T(1,128)S(1)}, u32[]{:S(2)}, u32[]{:S(2)}) async-start(f32[16,1,128]{2,1,0:T(1,128)} %broadcast_in_dim.79), calls=%async_computation.5 | async-start | bytes 16384 | tf_op jit(solution)/shard_map/all_to_all | solution.py:17
  160.9 6.9 %all-to-all-done.5 = f32[16,1,128]{2,1,0:T(1,128)S(1)} async-done(((f32[16,1,128]{2,1,0:T(1,128)}), f32[16,1,128]{2,1,0:T(1,128)S(1)}, u32[]{:S(2)}, u32[]{:S(2)}) %all-to-all-start.5) | async-done | bytes 8224 | tf_op jit(solution)/shard_map/all_to_all | solution.py:17
  167.8 1.1 broadcast_in_dim.77
  168.9 4.8 %all-to-all-start.4 = ((f32[16,129,128]{2,1,0:T(8,128)}), f32[16,129,128]{2,1,0:T(8,128)}, u32[]{:S(2)}, u32[]{:S(2)}) async-start(f32[16,129,128]{2,1,0:T(8,128)} %broadcast_in_dim.77), calls=%async_computation.4 | async-start | bytes 2228224 | tf_op jit(solution)/shard_map/all_to_all | solution.py:17
  174.5 13.7 %while.62 = (s32[]{:T(128)}, f32[1,128,128]{2,1,0:T(8,128)S(1)}, f32[4,1,256,128]{3,2,1,0:T(8,128)}, f32[1]{0:T(128)}, f32[4]{0:T(128)S(1)}, /*index=5*/f32[4,1,...) while((s32[]{:T(128)}, f32[1,128,128]{2,1,0:T(8,128)S(1)}, ...), condition=%wide.region_12.13_spmd.clone.clone.clone, body=%wide.region_11.12_spmd.clone.clone.clone.sunk | while | flops 302580480 | bytes 1908407 | solution.py:98
  180.4 1.0 fusion.251
  183.8 1.1 fusion.251
  189.1 1.3 copy.104
  190.5 1.2 copy.105
  192.6 3.6 %fusion.136 = bf16[1,1024,128]{2,1,0:T(8,128)(2,1)} fusion(f32[1024,128]{1,0:T(8,128)} %bitcast.423, f32[1024,128]{0,1:T(8,128)S(1)} %get-tuple-element.861, f32[1024]{0:T(1024)} %copy-done.13, f32[1024]{0:T(1024)S(1)} %get-tuple-element.844, f32[1024]{0:T(1024)} %copy-done.15, f32[128]{0:T(128)} %bitcast.437, f32[2,1,128,128]{3,2,1,0:T(8,128)S(1)} %copy-done.12, ...), kind=kOutput, calls=%fused_computation.164 | convolution fusion | flops 203194368 | bytes 1982980 | tf_op jit(solution)/shard_map/hle,hde->hld/dot_general | solution.py:172
  196.7 6.5 %all-to-all-done.4 = f32[16,129,128]{2,1,0:T(8,128)} async-done(((f32[16,129,128]{2,1,0:T(8,128)}), f32[16,129,128]{2,1,0:T(8,128)}, u32[]{:S(2)}, u32[]{:S(2)}) %all-to-all-start.4) | async-done | bytes 1056800 | tf_op jit(solution)/shard_map/all_to_all | solution.py:17
  204.4 1.4 fusion.137
  206.8 1.2 fusion.131
  209.7 1.3 fusion.129
  (207 shorter events, 53.0 us)
Async XLA Ops:
  0.6 4.7 %copy-start.4 = (bf16[1,1024,128]{2,1,0:T(8,128)(2,1)S(1)}, bf16[1,1024,128]{2,1,0:T(8,128)(2,1)}, u32[]{:S(2)}) copy-start(bf16[1,1024,128]{2,1,0:T(8,128)(2,1)} %param.16) | copy-start | bytes 786436
  18.4 17.7 %copy-start.10 = (bf16[1,1024,128]{2,1,0:T(8,128)(2,1)S(1)}, bf16[1,1024,128]{2,1,0:T(8,128)(2,1)}, u32[]{:S(2)}) copy-start(bf16[1,1024,128]{2,1,0:T(8,128)(2,1)} %param.20) | copy-start | bytes 786436
  18.4 47.1 %all-to-all-start = ((f32[16,129,128]{2,1,0:T(8,128)}), f32[16,129,128]{2,1,0:T(8,128)S(1)}, u32[]{:S(2)}, u32[]{:S(2)}) async-start(f32[16,129,128]{2,1,0:T(8,128)} %broadcast_in_dim.66), calls=%async_computation | async-start | bytes 2228224 | tf_op jit(solution)/shard_map/all_to_all | solution.py:17
  36.3 30.7 %copy-start = (bf16[1,1024,128]{1,2,0:T(8,128)(2,1)}, bf16[1,1024,128]{1,2,0:T(8,128)(2,1)S(1)}, u32[]{:S(2)}) copy-start(bf16[1,1024,128]{1,2,0:T(8,128)(2,1)S(1)} %copy.87) | copy-start | bytes 786436
  37.5 29.5 %copy-start.2 = (bf16[1,1024,128]{1,2,0:T(8,128)(2,1)}, bf16[1,1024,128]{1,2,0:T(8,128)(2,1)S(1)}, u32[]{:S(2)}) copy-start(bf16[1,1024,128]{1,2,0:T(8,128)(2,1)S(1)} %copy.83) | copy-start | bytes 786436
  39.4 27.7 %copy-start.15 = (f32[1024]{0:T(1024)}, f32[1024]{0:T(1024)S(1)}, u32[]{:S(2)}) copy-start(f32[1024]{0:T(1024)S(1)} %get-tuple-element.863) | copy-start | bytes 12292
  66.7 1.0 copy-start.5
  66.7 1.1 copy-start.9
  66.7 1.1 copy-start.14
  67.0 2.0 copy-start.11
  76.3 7.4 %all-to-all-start.1 = ((f32[4,1,1024]{2,1,0:T(1,128)}), f32[4,1,1024]{2,1,0:T(1,128)S(1)}, u32[]{:S(2)}, u32[]{:S(2)}) async-start(f32[4,1,1024]{2,1,0:T(1,128)} %broadcast_in_dim.70), calls=%async_computation.1 | async-start | bytes 32768 | tf_op jit(solution)/shard_map/all_to_all | solution.py:17
  79.5 15.9 %copy-start.6 = (bf16[1,1024,128]{2,1,0:T(8,128)(2,1)S(1)}, bf16[1,1024,128]{2,1,0:T(8,128)(2,1)}, u32[]{:S(2)}) copy-start(bf16[1,1024,128]{2,1,0:T(8,128)(2,1)} %param.18) | copy-start | bytes 786436
  84.5 23.0 %all-to-all-start.3 = ((f32[16,1,2048]{2,1,0:T(1,128)}), f32[16,1,2048]{2,1,0:T(1,128)S(1)}, u32[]{:S(2)}, u32[]{:S(2)}) async-start(f32[16,1,2048]{2,1,0:T(1,128)} %broadcast_in_dim.75), calls=%async_computation.3 | async-start | bytes 262144 | tf_op jit(solution)/shard_map/all_to_all | solution.py:17
  107.5 28.1 %copy-start.13 = (f32[1024]{0:T(1024)}, f32[1024]{0:T(1024)S(1)}, u32[]{:S(2)}) copy-start(f32[1024]{0:T(1024)S(1)} %get-tuple-element.843) | copy-start | bytes 12292
  153.2 14.6 %all-to-all-start.5 = ((f32[16,1,128]{2,1,0:T(1,128)}), f32[16,1,128]{2,1,0:T(1,128)S(1)}, u32[]{:S(2)}, u32[]{:S(2)}) async-start(f32[16,1,128]{2,1,0:T(1,128)} %broadcast_in_dim.79), calls=%async_computation.5 | async-start | bytes 16384 | tf_op jit(solution)/shard_map/all_to_all | solution.py:17
  168.9 34.2 %all-to-all-start.4 = ((f32[16,129,128]{2,1,0:T(8,128)}), f32[16,129,128]{2,1,0:T(8,128)}, u32[]{:S(2)}, u32[]{:S(2)}) async-start(f32[16,129,128]{2,1,0:T(8,128)} %broadcast_in_dim.77), calls=%async_computation.4 | async-start | bytes 2228224 | tf_op jit(solution)/shard_map/all_to_all | solution.py:17
  174.5 13.8 %copy-start.8 = (bf16[1,1024,128]{1,2,0:T(8,128)(2,1)S(1)}, bf16[1,1024,128]{1,2,0:T(8,128)(2,1)}, u32[]{:S(2)}) copy-start(bf16[1,1024,128]{1,2,0:T(8,128)(2,1)} %get-tuple-element.841) | copy-start | bytes 786436
  189.1 2.6 %copy-start.7 = (bf16[1,1024,128]{1,2,0:T(8,128)(2,1)S(1)}, bf16[1,1024,128]{1,2,0:T(8,128)(2,1)}, u32[]{:S(2)}) copy-start(bf16[1,1024,128]{1,2,0:T(8,128)(2,1)} %get-tuple-element.840) | copy-start | bytes 786436
  189.1 3.4 %copy-start.1 = (bf16[1,1024,128]{1,2,0:T(8,128)(2,1)S(1)}, bf16[1,1024,128]{1,2,0:T(8,128)(2,1)}, u32[]{:S(2)}) copy-start(bf16[1,1024,128]{1,2,0:T(8,128)(2,1)} %copy-done) | copy-start | bytes 786436
  189.1 3.4 %copy-start.3 = (bf16[1,1024,128]{1,2,0:T(8,128)(2,1)S(1)}, bf16[1,1024,128]{1,2,0:T(8,128)(2,1)}, u32[]{:S(2)}) copy-start(bf16[1,1024,128]{1,2,0:T(8,128)(2,1)} %copy-done.2) | copy-start | bytes 786436
  189.1 3.4 %copy-start.12 = (f32[2,1,128,128]{3,2,1,0:T(8,128)S(1)}, f32[2,1,128,128]{3,2,1,0:T(8,128)}, u32[]{:S(2)}) copy-start(f32[2,1,128,128]{3,2,1,0:T(8,128)} %copy-done.11) | copy-start | bytes 393220
  192.6 11.8 %copy-start.16 = (pred[16]{0:T(512)(128)(4,1)S(1)}, pred[16]{0:T(512)(128)(4,1)}, u32[]{:S(2)}) copy-start(pred[16]{0:T(512)(128)(4,1)} %iota_compare_fusion.2) | copy-start | bytes 52
where the time goes:
time: 214 us; the launch traced here: 213 us
  waiting for transfers between devices  48.3 us (23%)
  matrix products  46.5 us (22%)
  starting transfers between devices  44.4 us (21%)
  local copies, waits for them, and re-layouts  37.3 us (17%)
  other arithmetic  16.5 us (8%)
  loops' own time  10.6 us (5%)
  blocking collectives  6.56 us (3%)
  between operations  2.54 us (1%)
    all_to_all x5, waiting for transfers between devices, sent_to_all(): lax.all_to_all(jnp.broadcast_to(shard[None], (peers, *shard.shape)), axis...  48.3 us
    all_to_all x5, starting transfers between devices, sent_to_all(): lax.all_to_all(jnp.broadcast_to(shard[None], (peers, *shard.shape)), axis...  44.4 us
    dot_general x16, matrix products, advance(): jnp.dot(scores, value_part, precision=highest)  14.1 us
    another operation x4, loops' own time, run_blocks(): lax.scan(advance, initial, (query_blocks, key_blocks, value_blocks, block...  10.6 us
    dot_general x16, matrix products, advance(): scores = jnp.dot(query_part, key_part.T, precision=highest) * weights  9.77 us
    dynamic_slice x16, local copies, waits for them, and re-layouts, run_blocks(): lax.scan(advance, initial, (query_blocks, key_blocks, value_blocks, block...  9.37 us
    another operation x10, local copies, waits for them, and re-layouts  8.84 us
    dot_general x16, matrix products, advance(): jnp.dot(query_part, carried, precision=highest)  7.85 us
  transfers between devices with their start and end apart: 5, of which 5 were waited for; matrix products, arithmetic and copies ran while one was open for 14% of the time, Pallas kernels for 0%

commit v1 on v0

v1 whole, which is shorter than its diff:
```python
import math

import jax
import jax.numpy as jnp
from jax import lax
from jax.experimental import pallas as pl
from jax.experimental.pallas import tpu as pltpu
from jax.sharding import PartitionSpec as P

BLOCK = 256
EPSILON = 1e-06
F32 = jnp.float32
BF16 = jnp.bfloat16
WIDTH = 128
HALF = 64
LIMIT = 24 << 20


def split(x):
    high = x.astype(BF16)
    return high, (x - high.astype(F32)).astype(BF16)


def dot(a, b, da=1, db=0):
    return lax.dot_general(a, b, (((da,), (db,)), ((), ())), preferred_element_type=F32)


def dot_split(a, x, da=1):
    high, low = split(x)
    both = dot(a, jnp.concatenate([high, low], axis=1), da, 0)
    n = x.shape[1]
    return both[:, :n] + both[:, n:]


def rows_iota(rows, columns=WIDTH):
    return lax.broadcasted_iota(jnp.int32, (rows, columns), 0).astype(F32)


def decay_matrix(rate):
    at = lax.broadcasted_iota(jnp.int32, (BLOCK, BLOCK), 0)
    of = lax.broadcasted_iota(jnp.int32, (BLOCK, BLOCK), 1)
    distance = (at - of).astype(F32)
    return jnp.where(distance >= 0, jnp.exp(-rate * jnp.maximum(distance, 0.0)), 0.0)


def power(rate, tokens):
    return jnp.exp(jnp.full((1, WIDTH), -rate * tokens, F32))


def block_rows(b):
    return pl.ds(b * BLOCK, BLOCK)


def kept(flags_ref, b):
    return 1.0 - flags_ref[0, b].astype(F32)


def closing_kernel(rate_ref, flags_ref, k_ref, v_ref, own_ref, pairs_ref):
    rate = rate_ref[0]
    blocks = k_ref.shape[1] // BLOCK
    decay_out = jnp.exp(-rate * (float(BLOCK) - rows_iota(BLOCK)))
    over_block = power(rate, float(BLOCK))
    carried = jnp.zeros((WIDTH, WIDTH), F32)
    unbroken = 1.0
    for b in range(blocks):
        keep = kept(flags_ref, b)
        piece = dot_split(
            k_ref[0, block_rows(b)], decay_out * v_ref[0, block_rows(b)].astype(F32), 0
        )
        pairs_ref[b] = piece
        carried = carried * (over_block * keep) + piece
        unbroken = unbroken * keep
    own_ref[:WIDTH] = carried
    own_ref[WIDTH:] = jnp.full((8, WIDTH), unbroken, F32)


def local_kernel(rate_ref, q_ref, k_ref, v_ref, out_ref):
    weights = decay_matrix(rate_ref[0])
    for b in range(q_ref.shape[1] // BLOCK):
        rows = block_rows(b)
        scores = dot(q_ref[0, rows], k_ref[0, rows], 1, 1) * weights
        high, low = split(scores)
        v = v_ref[0, rows]
        out_ref[rows] = dot(high, v) + dot(low, v)


def forward_half_kernel(tokens, rate_ref, place_ref, own_ref, other_ref, out_ref):
    second = lax.rem(place_ref[0], 2) == 1
    over_slab = power(rate_ref[0], float(tokens))
    own, other = own_ref[:WIDTH], other_ref[:WIDTH]
    early = jnp.where(second, other, own)
    late = jnp.where(second, own, other)
    late_kept = jnp.where(second, own_ref[WIDTH : WIDTH + 1], other_ref[WIDTH : WIDTH + 1])
    chip = early * (late_kept * over_slab) + late
    out_ref[:HALF] = jnp.where(second, chip[HALF:], chip[:HALF])
    out_ref[HALF:] = own_ref[WIDTH:]


def backward_half_kernel(tokens, rate_ref, place_ref, own_ref, other_ref, gain_ref, unbroken_ref, out_ref):
    place = place_ref[0]
    second = lax.rem(place, 2) == 1
    over_slab = power(rate_ref[0], float(tokens))
    own, other = own_ref[...], other_ref[...]
    early = jnp.where(second, other, own)
    late = jnp.where(second, own, other)
    early_kept = unbroken_ref[pl.ds(place - lax.rem(place, 2), 1)]
    chip = late * (early_kept * over_slab) + early
    out_ref[:HALF] = jnp.where(second, chip[HALF:], chip[:HALF])
    out_ref[HALF:] = jnp.broadcast_to(gain_ref[...], (8, WIDTH))


def chip_state(all_ref, c):
    return jnp.concatenate([all_ref[2 * c, :HALF], all_ref[2 * c + 1, :HALF]], axis=0)


def attended_kernel(
    tokens,
    rate_ref,
    flags_ref,
    place_ref,
    all_ref,
    other_ref,
    pairs_ref,
    q_ref,
    local_ref,
    gate_ref,
    cotangent_ref,
    gain_ref,
    attended_ref,
    states_ref,
    sums_ref,
    unbroken_ref,
):
    rate = rate_ref[0]
    place = place_ref[0]
    chip, core = place // 2, lax.rem(place, 2)
    over_slab = power(rate, float(tokens))
    slabs = all_ref.shape[0]
    state = jnp.zeros((WIDTH, WIDTH), F32)
    for c in range(slabs // 2):
        before = c < chip
        factor = all_ref[2 * c, HALF : HALF + 1] * all_ref[2 * c + 1, HALF : HALF + 1]
        state = jnp.where(
            before, state * (factor * over_slab * over_slab) + chip_state(all_ref, c), state
        )
    state = jnp.where(
        core == 1,
        state * (other_ref[WIDTH : WIDTH + 1] * over_slab) + other_ref[:WIDTH],
        state,
    )
    for s in range(slabs):
        unbroken_ref[s : s + 1] = all_ref[s, HALF : HALF + 1]
    decay_in = jnp.exp(-rate * rows_iota(BLOCK))
    over_block = power(rate, float(BLOCK))
    ones = jnp.ones((8, WIDTH), BF16)
    first = lax.broadcasted_iota(jnp.int32, (8, BLOCK), 0) == 0
    for b in range(tokens // BLOCK):
        rows = block_rows(b)
        state = state * kept(flags_ref, b)
        states_ref[b] = state
        attended = local_ref[rows] + decay_in * dot_split(q_ref[0, rows], state)
        attended_ref[rows] = attended
        opening = jax.nn.sigmoid(gate_ref[0, rows].astype(F32))
        grad_norm = cotangent_ref[0, rows].astype(F32) * opening * gain_ref[...]
        sq_high, sq_low = split(attended * attended)
        cross_high, cross_low = split(grad_norm * attended)
        squares = dot(ones, sq_high, 1, 1) + dot(ones, sq_low, 1, 1)
        crosses = dot(ones, cross_high, 1, 1) + dot(ones, cross_low, 1, 1)
        both = jnp.where(first, squares, crosses)[:2]
        for p in range(sums_ref.shape[0]):
            sums_ref[p, :, b * BLOCK : (b + 1) * BLOCK] = both
        state = state * over_block + pairs_ref[b]


def spread_kernel(parts_ref, out_ref):
    total = parts_ref[0]
    for p in range(1, parts_ref.shape[0]):
        total = total + parts_ref[p]
    for p in range(out_ref.shape[0]):
        out_ref[p] = total


def thirds(row):
    high = row.astype(BF16).astype(F32)
    rest = row - high
    middle = rest.astype(BF16).astype(F32)
    return high, middle, rest - middle


def columns_of(first, second):
    pieces = thirds(first) + thirds(second)
    n = first.shape[1]
    at = lax.broadcasted_iota(jnp.int32, (16, n), 0)
    stacked = jnp.zeros((16, n), F32)
    for i, piece in enumerate(pieces):
        stacked = jnp.where(at == i, piece, stacked)
    row = lax.broadcasted_iota(jnp.int32, (16, 2 * WIDTH), 0)
    column = lax.broadcasted_iota(jnp.int32, (16, 2 * WIDTH), 1)
    chosen = jnp.where((row >= 3) == (column >= WIDTH), 1.0, 0.0).astype(BF16)
    both = dot(stacked.astype(BF16), chosen, 0, 0)
    return both[:, :WIDTH], both[:, WIDTH:]


def grad_kernel(
    features,
    row_total,
    rate_ref,
    flags_ref,
    parts_ref,
    attended_ref,
    q_ref,
    gate_ref,
    cotangent_ref,
    gain_ref,
    own_ref,
    gain_part_ref,
    high_ref,
    low_ref,
    pieces_ref,
    inverse_ref,
):
    rate = rate_ref[0]
    total = parts_ref[0]
    for p in range(1, parts_ref.shape[0]):
        total = total + parts_ref[p]
    inverse_row = lax.rsqrt(total[0:1] * (1.0 / features) + EPSILON)
    slope_row = inverse_row * total[1:2] * (1.0 / features)
    decay_on = jnp.exp(-rate * (rows_iota(BLOCK) + 1.0))
    over_block = power(rate, float(BLOCK))
    carried = jnp.zeros((WIDTH, WIDTH), F32)
    gain_sum = jnp.zeros((1, WIDTH), F32)
    for b in reversed(range(q_ref.shape[1] // BLOCK)):
        rows = block_rows(b)
        lanes = slice(b * BLOCK, (b + 1) * BLOCK)
        inverse, slope = columns_of(inverse_row[:, lanes], slope_row[:, lanes])
        inverse_ref[rows] = inverse
        normed = attended_ref[rows] * inverse
        opening = jax.nn.sigmoid(gate_ref[0, rows].astype(F32))
        grad_open = cotangent_ref[0, rows].astype(F32) * opening
        gain_sum = gain_sum + jnp.sum(grad_open * normed, axis=0, keepdims=True)
        grad = inverse * (grad_open * gain_ref[...] - normed * slope)
        high, low = split(grad)
        high_ref[rows] = high
        low_ref[rows] = low
        piece = dot_split(q_ref[0, rows], decay_on * grad, 0)
        pieces_ref[b] = piece
        carried = (carried * over_block + piece) * kept(flags_ref, b)
    own_ref[...] = carried
    gain_part_ref[...] = gain_sum * (1.0 / math.sqrt(row_total))


def backward_kernel(
    rate_ref,
    q_ref,
    k_ref,
    v_ref,
    gate_ref,
    cotangent_ref,
    gain_ref,
    high_ref,
    low_ref,
    inverse_ref,
    attended_ref,
    states_ref,
    mixed_ref,
    gate_grad_ref,
    query_grad_ref,
    key_part_ref,
    value_part_ref,
):
    rate = rate_ref[0]
    weights = decay_matrix(rate)
    decay_in = jnp.exp(-rate * rows_iota(BLOCK))
    for b in range(q_ref.shape[1] // BLOCK):
        rows = block_rows(b)
        q, k, v = q_ref[0, rows], k_ref[0, rows], v_ref[0, rows]
        high, low = high_ref[rows], low_ref[rows]
        normed = attended_ref[rows] * inverse_ref[rows]
        opening = jax.nn.sigmoid(gate_ref[0, rows].astype(F32))
        mixed = opening * gain_ref[...] * normed
        mixed_ref[0, rows] = mixed.astype(BF16)
        gate_grad_ref[0, rows] = (
            cotangent_ref[0, rows].astype(F32) * mixed * (1.0 - opening)
        ).astype(BF16)
        slopes = (dot(high, v, 1, 1) + dot(low, v, 1, 1)) * weights
        slopes_high, slopes_low = split(slopes)
        state_high, state_low = split(states_ref[b])
        across = dot(high, state_high, 1, 1) + dot(high, state_low, 1, 1) + dot(low, state_high, 1, 1)
        query_grad_ref[0, rows] = (
            dot(slopes_high, k) + dot(slopes_low, k) + decay_in * across
        ).astype(BF16)
        key_part_ref[rows] = dot(slopes_high, q, 0, 0) + dot(slopes_low, q, 0, 0)
        scores_high, scores_low = split(dot(q, k, 1, 1) * weights)
        both = dot(scores_high, jnp.concatenate([high, low], axis=1), 0, 0)
        value_part_ref[rows] = both[:, :WIDTH] + both[:, WIDTH:] + dot(scores_low, high, 0, 0)


def finish_kernel(
    tokens,
    rate_ref,
    flags_ref,
    place_ref,
    all_ref,
    other_ref,
    unbroken_ref,
    pieces_ref,
    k_ref,
    v_ref,
    key_part_ref,
    value_part_ref,
    key_grad_ref,
    value_grad_ref,
    gain_grad_ref,
):
    rate = rate_ref[0]
    place = place_ref[0]
    chip, core = place // 2, lax.rem(place, 2)
    over_slab = power(rate, float(tokens))
    slabs = all_ref.shape[0]
    state = jnp.zeros((WIDTH, WIDTH), F32)
    for c in reversed(range(slabs // 2)):
        after = c > chip
        factor = unbroken_ref[2 * c : 2 * c + 1] * unbroken_ref[2 * c + 1 : 2 * c + 2]
        state = jnp.where(
            after, state * (factor * over_slab * over_slab) + chip_state(all_ref, c), state
        )
    partner = unbroken_ref[pl.ds(place - core + 1, 1)]
    state = jnp.where(core == 0, state * (partner * over_slab) + other_ref[...], state)
    gain = all_ref[0, HALF : HALF + 1]
    for s in range(1, slabs):
        gain = gain + all_ref[s, HALF : HALF + 1]
    gain_grad_ref[...] = gain
    decay_back = jnp.exp(-rate * (float(BLOCK - 1) - rows_iota(BLOCK)))
    over_block = power(rate, float(BLOCK))
    last = tokens // BLOCK - 1
    for b in reversed(range(last + 1)):
        rows = block_rows(b)
        if b < last:
            state = state * kept(flags_ref, b + 1)
        high, low = split(state)
        k, v = k_ref[0, rows], v_ref[0, rows]
        both = dot(k, jnp.concatenate([high, low], axis=1))
        value_grad_ref[0, rows] = (
            value_part_ref[rows] + decay_back * (both[:, :WIDTH] + both[:, WIDTH:])
        ).astype(BF16)
        both = dot(v, jnp.concatenate([high, low], axis=0), 1, 1)
        key_grad_ref[0, rows] = (
            key_part_ref[rows] + decay_back * (both[:, :WIDTH] + both[:, WIDTH:])
        ).astype(BF16)
        state = state * over_block + pieces_ref[b]


def call(kernel, scalars, arrays, outs, flops=1 << 24):
    smem = pl.BlockSpec(memory_space=pltpu.SMEM)
    vmem = pl.BlockSpec(memory_space=pltpu.VMEM)
    moved = sum(a.size * a.dtype.itemsize for a in (*arrays, *outs))
    return pl.pallas_call(
        kernel,
        out_shape=outs,
        in_specs=[smem] * len(scalars) + [vmem] * len(arrays),
        out_specs=[vmem] * len(outs),
        compiler_params=pltpu.CompilerParams(vmem_limit_bytes=LIMIT),
        cost_estimate=pl.CostEstimate(flops=flops, bytes_accessed=moved, transcendentals=0),
    )(*scalars, *arrays)


def shape(*dims, dtype=F32):
    return jax.ShapeDtypeStruct(dims, dtype)


def bound(kernel, *fixed):
    def run(*refs):
        kernel(*fixed, *refs)

    return run


def body(queries, key_tokens, values, gate_logits, cotangent, decay_rates, norm_gain, block_starts):
    tokens = queries.shape[1]
    blocks = tokens // BLOCK
    slabs = lax.axis_size("ctx")
    outer, inner = lax.axis_size("dp"), lax.axis_size("pipe")
    features = float(WIDTH * outer * inner)
    place = lax.axis_index("ctx").astype(jnp.int32).reshape(1)
    partners = [(j, j ^ 1) for j in range(slabs)]
    like = shape(1, tokens, WIDTH, dtype=BF16)
    wide = shape(tokens, WIDTH)
    states = shape(blocks, WIDTH, WIDTH)

    own, pairs = call(
        closing_kernel,
        (decay_rates, block_starts),
        (key_tokens, values),
        [shape(WIDTH + 8, WIDTH), states],
    )
    other = lax.ppermute(own, "ctx", partners)
    (local,) = call(
        local_kernel, (decay_rates,), (queries, key_tokens, values), [wide], flops=1 << 28
    )
    (half,) = call(
        bound(forward_half_kernel, tokens),
        (decay_rates, place),
        (own, other),
        [shape(HALF + 8, WIDTH)],
    )
    everyone = lax.all_gather(half, "ctx")
    attended, states_in, sums, unbroken = call(
        bound(attended_kernel, tokens),
        (decay_rates, block_starts, place),
        (everyone, other, pairs, queries, local, gate_logits, cotangent, norm_gain),
        [wide, states, shape(inner, 2, tokens), shape(slabs, WIDTH)],
    )
    sums = lax.all_to_all(sums, "pipe", 0, 0, tiled=True)
    (sums,) = call(spread_kernel, (), (sums,), [shape(outer, 2, tokens)])
    sums = lax.all_to_all(sums, "dp", 0, 0, tiled=True)
    back, gain_part, high, low, pieces, inverse = call(
        bound(grad_kernel, features, tokens * slabs),
        (decay_rates, block_starts),
        (sums, attended, queries, gate_logits, cotangent, norm_gain),
        [
            shape(WIDTH, WIDTH),
            shape(1, WIDTH),
            shape(tokens, WIDTH, dtype=BF16),
            shape(tokens, WIDTH, dtype=BF16),
            states,
            wide,
        ],
    )
    back_other = lax.ppermute(back, "ctx", partners)
    mixed_out, gate_grad, query_grad, key_part, value_part = call(
        backward_kernel,
        (decay_rates,),
        (
            queries,
            key_tokens,
            values,
            gate_logits,
            cotangent,
            norm_gain,
            high,
            low,
            inverse,
            attended,
            states_in,
        ),
        [like, like, like, wide, wide],
        flops=1 << 30,
    )
    (back_half,) = call(
        bound(backward_half_kernel, tokens),
        (decay_rates, place),
        (back, back_other, gain_part, unbroken),
        [shape(HALF + 8, WIDTH)],
    )
    back_everyone = lax.all_gather(back_half, "ctx")
    key_grad, value_grad, gain_grad = call(
        bound(finish_kernel, tokens),
        (decay_rates, block_starts, place),
        (
            back_everyone,
            back_other,
            unbroken,
            pieces,
            key_tokens,
            values,
            key_part,
            value_part,
        ),
        [like, like, shape(1, WIDTH)],
    )
    return (mixed_out, query_grad, key_grad, value_grad, gate_grad, gain_grad)


def solution(mesh):
    wide = P(None, "ctx", ("dp", "pipe"))
    heads = P(("dp", "pipe"))
    gain = P(("dp", "pipe"), None)
    return jax.shard_map(
        body,
        mesh=mesh,
        in_specs=(wide, wide, wide, wide, wide, heads, gain, P(None, "ctx")),
        out_specs=(wide, wide, wide, wide, wide, gain),
        check_vma=False,
    )
```

time: 214 us -> 99.7 us (0.47)
  blocking collectives: 6.56 us -> 61.4 us
  waiting for transfers between devices: 48.3 us -> 0.01 us
  matrix products: 46.5 us -> 0 us
  local copies, waits for them, and re-layouts: 37.3 us -> 3.51 us
  starting transfers between devices: 44.4 us -> 21.9 us
  other arithmetic: 16.5 us -> 0 us
  Pallas kernels: 0 us -> 11 us
  loops' own time: 10.6 us -> 0 us
    all_to_all x5 -> x0, waiting for transfers between devices: 48.3 us -> none  [sent_to_all(): lax.all_to_all(jnp.broadcast_to(shard[None], (peers, *shard.shape)), axis...]
    dot_general x68 -> x0, matrix products: 46.5 us -> none  [the longest x16 14.1 us: advance(): jnp.dot(scores, value_part, precision=highest)]
    all_to_all x5 -> x0, starting transfers between devices: 44.4 us -> none  [sent_to_all(): lax.all_to_all(jnp.broadcast_to(shard[None], (peers, *shard.shape)), axis...]
    all_gather x0 -> x2, blocking collectives: none -> 32.6 us  [the longest x1 16.4 us: body(): back_everyone = lax.all_gather(back_half, 'ctx')]
    all_to_all x1 -> x2, blocking collectives: 6.56 us -> 28.8 us  [the longest x1 22.2 us: body(): sums = lax.all_to_all(sums, 'dp', 0, 0, tiled=True)]
    ppermute x0 -> x2, starting transfers between devices: none -> 21.9 us  [the longest x1 16 us: body(): other = lax.ppermute(own, 'ctx', partners)]
    pallas_call x0 -> x9, Pallas kernels: none -> 11 us  [call(): pl.pallas_call(kernel, out_shape=outs, in_specs=[smem] * len(scalars) + [...]
    another operation x4 -> x0, loops' own time: 10.6 us -> none  [run_blocks(): lax.scan(advance, initial, (query_blocks, key_blocks, value_blocks, block...]
  transfers between devices with their start and end apart: 5 -> 2, of which waited for: 5 -> 0; matrix products, arithmetic and copies ran while one was open for 14% -> 0% of each run, Pallas kernels for 0% -> 5%
where the time goes in v1:
time: 99.7 us; the launch traced here: 99.4 us
  blocking collectives  61.4 us (62%)
  starting transfers between devices  21.9 us (22%)
  Pallas kernels  11 us (11%)
  local copies, waits for them, and re-layouts  3.51 us (4%)
  between operations  1.44 us (1%)
    all_to_all x1, blocking collectives, body(): sums = lax.all_to_all(sums, 'dp', 0, 0, tiled=True)  22.2 us
    all_gather x1, blocking collectives, body(): back_everyone = lax.all_gather(back_half, 'ctx')  16.4 us
    all_gather x1, blocking collectives, body(): everyone = lax.all_gather(half, 'ctx')  16.2 us
    ppermute x1, starting transfers between devices, body(): other = lax.ppermute(own, 'ctx', partners)  16 us
    pallas_call x9, Pallas kernels, call(): pl.pallas_call(kernel, out_shape=outs, in_specs=[smem] * len(scalars) + [...  11 us
    all_to_all x1, blocking collectives, body(): sums = lax.all_to_all(sums, 'pipe', 0, 0, tiled=True)  6.66 us
    ppermute x1, starting transfers between devices, body(): back_other = lax.ppermute(back, 'ctx', partners)  5.93 us
    unnamed x20, local copies, waits for them, and re-layouts  3.51 us
  transfers between devices with their start and end apart: 2, of which 0 were waited for; matrix products, arithmetic and copies ran while one was open for 0% of the time, Pallas kernels for 5%

profile of v1, /device:TPU:1, one launch (start us, length us, event | category | flops | bytes accessed | tf_op | source)
XLA Modules:
  0.0 99.4 jit_solution(17044516167718157789)
XLA Ops:
  0.6 0.0 copy-start.8
  1.3 0.0 copy-done.8
  1.3 0.0 copy-start
  1.3 0.9 copy-done
  2.3 0.0 copy-start.2
  2.3 0.9 copy-done.2
  3.2 0.0 copy-start.1
  3.2 0.0 copy-start.3
  3.2 0.8 shard_map.127
  4.0 16.0 %collective-permute-start = (f32[136,128]{1,0:T(8,128)S(1)}, f32[136,128]{1,0:T(8,128)S(1)}, u32[]{:S(2)}, u32[]{:S(2)}) collective-permute-start(f32[136,128]{1,0:T(8,128)S(1)} %get-tuple-element.26.refs_2_), channel_id=1, source_target_pairs={{0,64},{64,0},{128,192},{192,128},{256,320},{320,256},{384,448},{4... | collective-permute-start | bytes 208904 | tf_op jit(solution)/shard_map/ppermute | solution.py:396
  20.1 0.0 copy-done.1
  20.1 0.0 copy-done.3
  20.1 0.0 copy-start.4
  20.1 0.9 copy-done.4
  21.1 0.9 shard_map.129.refs_7_
  22.0 0.0 collective-permute-done.refs_3_.refs_4_
  22.0 0.0 copy-start.7
  22.0 0.0 copy-start.5
  22.0 0.0 copy-start.6
  22.0 16.2 %all-gather = f32[1152,128]{1,0:T(8,128)S(1)} all-gather(f32[72,128]{1,0:T(8,128)S(1)} %shard_map.128), channel_id=2, replica_groups=mesh['ctx'=16,'dp'=16,'pipe'=4] {'ctx'}, dimensions={0}, use_global_device_ids=true | all-gather | bytes 626688 | tf_op jit(solution)/shard_map/all_gather | solution.py:406
  38.3 0.0 copy-start.9
  38.3 0.0 copy-done.7
  38.3 0.0 copy-done.5
  38.3 0.0 copy-done.6
  38.3 0.6 copy-done.9
  38.9 1.7 %shard_map.130 = (f32[1024,128]{1,0:T(8,128)S(1)}, f32[4,128,128]{2,1,0:T(8,128)S(1)}, f32[4,2,1024]{2,1,0:T(2,128)S(1)}, f32[16,128]{1,0:T(8,128)S(1)}) custom-call(f32[1]{0:T(128)S(6)} %copy.14.rate_ref.refs_0_, s32[1,4]{1,0:T(1,128)S(1)} %copy-done.8, s32[1]{0:T(128)} %bitcast.refs_1_.refs_2_, f32[16,72,128]{2,1,0:T(8,128)S(1)} %bitcast.4, ...), custom_call_target="tpu_custom_call" | custom-call | flops 16777216 | bytes 3060224 | tf_op jit(solution)/shard_map/pallas_call | solution.py:357
  40.6 6.7 %all_to_all.10.parts_ref = f32[4,2,1024]{2,1,0:T(2,128)S(1)} all-to-all(f32[4,2,1024]{2,1,0:T(2,128)S(1)} %get-tuple-element.28), channel_id=1, replica_groups=mesh['ctx'=16,'dp'=16,'pipe'=4] {'pipe'}, dimensions={0} | all-to-all | bytes 65536 | tf_op jit(solution)/shard_map/all_to_all | solution.py:413
  47.3 22.2 %all_to_all.11.refs_2_ = f32[16,2,1024]{2,1,0:T(2,128)S(1)} all-to-all(f32[16,2,1024]{2,1,0:T(2,128)S(1)} %shard_map.131), channel_id=1, replica_groups=mesh['ctx'=16,'dp'=16,'pipe'=4] {'dp'}, dimensions={0} | all-to-all | bytes 262144 | tf_op jit(solution)/shard_map/all_to_all | solution.py:415
  69.5 1.7 %shard_map.132 = (f32[128,128]{1,0:T(8,128)S(1)}, f32[1,128]{1,0:T(1,128)S(1)}, bf16[1024,128]{1,0:T(8,128)(2,1)S(1)}, bf16[1024,128]{1,0:T(8,128)(2,1)S(1)}, f3...) custom-call(f32[1]{0:T(128)S(6)} %copy.14.rate_ref.refs_0_, s32[1,4]{1,0:T(1,128)S(1)} %copy-done.8, ...), custom_call_target="tpu_custom_call" | custom-call | flops 16777216 | bytes 2819072 | tf_op jit(solution)/shard_map/pallas_call | solution.py:357
  71.1 5.9 %collective-permute-start.1 = (f32[128,128]{1,0:T(8,128)S(1)}, f32[128,128]{1,0:T(8,128)S(1)}, u32[]{:S(2)}, u32[]{:S(2)}) collective-permute-start(f32[128,128]{1,0:T(8,128)S(1)} %get-tuple-element.36.refs_2_), channel_id=1, source_target_pairs={{0,64},{64,0},{128,192},{192,128},{256,320},{320,256},{384,448},{4... | collective-permute-start | bytes 196616 | tf_op jit(solution)/shard_map/ppermute | solution.py:429
  77.1 4.0 %shard_map.133 = (bf16[1,1024,128]{2,1,0:T(8,128)(2,1)}, bf16[1,1024,128]{2,1,0:T(8,128)(2,1)}, bf16[1,1024,128]{2,1,0:T(8,128)(2,1)}, f32[1024,128]{1,0:T(8,128)S(1)}, f32[1024,128]{1,0:T(8,128)S(1)}) custom-call(f32[1]{0:T(128)S(6)} %copy.14.rate_ref.refs_0_, bf16[1,1024,128]{2,1,0:T(8,128)(2,1)S(1)} %copy-done.5, bf16[1,1024,128]{2,1,0:T(8,128)(2,1)S(1)} %copy-done.1, ...), custom_call_target="tpu_custom_call" | custom-call | flops 1073741824 | bytes 4981248 | tf_op jit(solution)/shard_map/pallas_call | solution.py:357
  81.1 0.0 collective-permute-done.1.refs_3_.refs_4_
  81.1 16.4 %all-gather.1 = f32[1152,128]{1,0:T(8,128)S(1)} all-gather(f32[72,128]{1,0:T(8,128)S(1)} %shard_map.134), channel_id=3, replica_groups=mesh['ctx'=16,'dp'=16,'pipe'=4] {'ctx'}, dimensions={0}, use_global_device_ids=true | all-gather | bytes 626688 | tf_op jit(solution)/shard_map/all_gather | solution.py:455
  97.5 1.8 %shard_map.135 = (bf16[1,1024,128]{2,1,0:T(8,128)(2,1)}, bf16[1,1024,128]{2,1,0:T(8,128)(2,1)}, f32[1,128]{1,0:T(1,128)}) custom-call(f32[1]{0:T(128)S(6)} %copy.14.rate_ref.refs_0_, s32[1,4]{1,0:T(1,128)S(1)} %copy-done.8, s32[1]{0:T(128)} %bitcast.refs_1_.refs_2_, f32[16,72,128]{2,1,0:T(8,128)S(1)} %bitcast.3, ...), custom_call_target="tpu_custom_call" | custom-call | flops 16777216 | bytes 3023360 | tf_op jit(solution)/shard_map/pallas_call | solution.py:357
  (3 shorter events, 0.1 us)
Async XLA Ops:
  0.6 0.7 copy-start.8
  1.3 1.0 copy-start
  2.3 0.9 copy-start.2
  3.2 16.9 %copy-start.1 = (bf16[1,1024,128]{2,1,0:T(8,128)(2,1)S(1)}, bf16[1,1024,128]{2,1,0:T(8,128)(2,1)}, u32[]{:S(2)}) copy-start(bf16[1,1024,128]{2,1,0:T(8,128)(2,1)} %refs_7_.3) | copy-start | bytes 786436
  3.2 16.9 %copy-start.3 = (bf16[1,1024,128]{2,1,0:T(8,128)(2,1)S(1)}, bf16[1,1024,128]{2,1,0:T(8,128)(2,1)}, u32[]{:S(2)}) copy-start(bf16[1,1024,128]{2,1,0:T(8,128)(2,1)} %refs_8_.3) | copy-start | bytes 786436
  4.0 17.9 %collective-permute-start = (f32[136,128]{1,0:T(8,128)S(1)}, f32[136,128]{1,0:T(8,128)S(1)}, u32[]{:S(2)}, u32[]{:S(2)}) collective-permute-start(f32[136,128]{1,0:T(8,128)S(1)} %get-tuple-element.26.refs_2_), channel_id=1, source_target_pairs={{0,64},{64,0},{128,192},{192,128},{256,320},{320,256},{384,448},{4... | collective-permute-start | bytes 208904 | tf_op jit(solution)/shard_map/ppermute | solution.py:396
  20.1 1.0 copy-start.4
  22.0 16.3 %copy-start.7 = (bf16[1,1024,128]{2,1,0:T(8,128)(2,1)S(1)}, bf16[1,1024,128]{2,1,0:T(8,128)(2,1)}, u32[]{:S(2)}) copy-start(bf16[1,1024,128]{2,1,0:T(8,128)(2,1)} %cotangent_ref.1) | copy-start | bytes 786436
  22.0 16.2 %copy-start.5 = (bf16[1,1024,128]{2,1,0:T(8,128)(2,1)S(1)}, bf16[1,1024,128]{2,1,0:T(8,128)(2,1)}, u32[]{:S(2)}) copy-start(bf16[1,1024,128]{2,1,0:T(8,128)(2,1)} %q_ref.3) | copy-start | bytes 786436
  22.0 16.2 %copy-start.6 = (bf16[1,1024,128]{2,1,0:T(8,128)(2,1)S(1)}, bf16[1,1024,128]{2,1,0:T(8,128)(2,1)}, u32[]{:S(2)}) copy-start(bf16[1,1024,128]{2,1,0:T(8,128)(2,1)} %gate_ref.1) | copy-start | bytes 786436
  38.3 0.7 copy-start.9
  71.1 10.0 %collective-permute-start.1 = (f32[128,128]{1,0:T(8,128)S(1)}, f32[128,128]{1,0:T(8,128)S(1)}, u32[]{:S(2)}, u32[]{:S(2)}) collective-permute-start(f32[128,128]{1,0:T(8,128)S(1)} %get-tuple-element.36.refs_2_), channel_id=1, source_target_pairs={{0,64},{64,0},{128,192},{192,128},{256,320},{320,256},{384,448},{4... | collective-permute-start | bytes 196616 | tf_op jit(solution)/shard_map/ppermute | solution.py:429

commit v2 on v1

v2 whole, which is shorter than its diff:
```python
import math

import jax
import jax.numpy as jnp
from jax import lax
from jax.experimental import pallas as pl
from jax.experimental.pallas import tpu as pltpu
from jax.sharding import PartitionSpec as P

BLOCK = 256
EPSILON = 1e-06
F32 = jnp.float32
BF16 = jnp.bfloat16
WIDTH = 128
HALF = 64
LIMIT = 12 << 20


def split(x):
    high = x.astype(BF16)
    return high, (x - high.astype(F32)).astype(BF16)


def dot(a, b, da=1, db=0):
    return lax.dot_general(a, b, (((da,), (db,)), ((), ())), preferred_element_type=F32)


def dot_split(a, x, da=1):
    high, low = split(x)
    both = dot(a, jnp.concatenate([high, low], axis=1), da, 0)
    n = x.shape[1]
    return both[:, :n] + both[:, n:]


def rows_iota(rows, columns=WIDTH):
    return lax.broadcasted_iota(jnp.int32, (rows, columns), 0).astype(F32)


def power(facts_ref, tokens):
    return jnp.exp(-rate_row(facts_ref) * tokens)


def rate_row(facts_ref):
    return facts_ref[0:1, :WIDTH]


def kept(facts_ref, b):
    return facts_ref[b + 1 : b + 2, :WIDTH]


def block_rows(b):
    return pl.ds(b * BLOCK, BLOCK)


def decay_matrix(facts_ref, at_axis=0):
    at = lax.broadcasted_iota(jnp.int32, (BLOCK, BLOCK), at_axis)
    of = lax.broadcasted_iota(jnp.int32, (BLOCK, BLOCK), 1 - at_axis)
    distance = (at - of).astype(F32)
    return jnp.where(
        distance >= 0, jnp.exp(-facts_ref[0:1] * jnp.maximum(distance, 0.0)), 0.0
    )


def halves(both):
    return both[:, :WIDTH] + both[:, WIDTH:]


def beside(a, b):
    return jnp.concatenate([a, b], axis=1)


def closing_kernel(
    rate_ref,
    flags_hbm,
    k_hbm,
    v_hbm,
    q_hbm,
    gain_hbm,
    own_ref,
    pairs_ref,
    facts_ref,
    k_ref,
    v_ref,
    q_ref,
    gain_ref,
    flags_smem,
    sems,
):
    blocks = k_ref.shape[0] // BLOCK
    flags_copy = pltpu.make_async_copy(flags_hbm, flags_smem, sems.at[0])
    flags_copy.start()
    parts = []
    for b in range(blocks):
        rows = block_rows(b)
        parts.append(
            [
                pltpu.make_async_copy(k_hbm.at[0, rows], k_ref.at[rows], sems.at[1 + 2 * b]),
                pltpu.make_async_copy(v_hbm.at[0, rows], v_ref.at[rows], sems.at[2 + 2 * b]),
            ]
        )
        for copy in parts[b]:
            copy.start()
    at = 1 + 2 * blocks
    rest = [
        pltpu.make_async_copy(q_hbm.at[0], q_ref, sems.at[at]),
        pltpu.make_async_copy(gain_hbm, gain_ref, sems.at[at + 1]),
    ]
    for copy in rest:
        copy.start()
    flags_copy.wait()
    facts_ref[0:1] = jnp.full((1, BLOCK), rate_ref[0], F32)
    unbroken = 1.0
    for b in range(blocks):
        keep = 1.0 - flags_smem[0, b].astype(F32)
        unbroken = unbroken * keep
        facts_ref[b + 1 : b + 2] = jnp.full((1, BLOCK), keep, F32)
    decay_out = jnp.exp(-rate_row(facts_ref) * (float(BLOCK) - rows_iota(BLOCK)))
    over_block = power(facts_ref, float(BLOCK))
    carried = jnp.zeros((WIDTH, WIDTH), F32)
    for b in range(blocks):
        for copy in parts[b]:
            copy.wait()
        rows = block_rows(b)
        piece = dot_split(k_ref[rows], decay_out * v_ref[rows].astype(F32), 0)
        pairs_ref[b] = piece
        carried = carried * (over_block * kept(facts_ref, b)) + piece
    own_ref[:WIDTH] = carried
    own_ref[WIDTH:] = jnp.full((8, WIDTH), unbroken, F32)
    for copy in rest:
        copy.wait()


def local_kernel(facts_ref, q_ref, k_ref, v_ref, out_ref):
    weights = decay_matrix(facts_ref)
    for b in range(q_ref.shape[0] // BLOCK):
        rows = block_rows(b)
        scores = dot(q_ref[rows], k_ref[rows], 1, 1) * weights
        high, low = split(scores)
        v = v_ref[rows]
        out_ref[rows] = dot(high, v) + dot(low, v)


def forward_half_kernel(tokens, place_ref, facts_ref, own_ref, other_ref, out_ref):
    second = lax.rem(place_ref[0], 2) == 1
    over_slab = power(facts_ref, float(tokens))
    own, other = own_ref[:WIDTH], other_ref[:WIDTH]
    early = jnp.where(second, other, own)
    late = jnp.where(second, own, other)
    late_kept = jnp.where(second, own_ref[WIDTH : WIDTH + 1], other_ref[WIDTH : WIDTH + 1])
    chip = early * (late_kept * over_slab) + late
    out_ref[:HALF] = jnp.where(second, chip[HALF:], chip[:HALF])
    out_ref[HALF:] = own_ref[WIDTH:]


def backward_half_kernel(
    tokens, place_ref, facts_ref, own_ref, other_ref, gain_ref, unbroken_ref, out_ref
):
    place = place_ref[0]
    second = lax.rem(place, 2) == 1
    over_slab = power(facts_ref, float(tokens))
    own, other = own_ref[...], other_ref[...]
    early = jnp.where(second, other, own)
    late = jnp.where(second, own, other)
    early_kept = unbroken_ref[pl.ds(place - lax.rem(place, 2), 1)]
    chip = late * (early_kept * over_slab) + early
    out_ref[:HALF] = jnp.where(second, chip[HALF:], chip[:HALF])
    out_ref[HALF:] = jnp.broadcast_to(gain_ref[...], (8, WIDTH))


def chip_state(all_ref, c):
    return jnp.concatenate([all_ref[2 * c, :HALF], all_ref[2 * c + 1, :HALF]], axis=0)


def attended_kernel(
    tokens,
    place_ref,
    facts_ref,
    all_ref,
    other_ref,
    pairs_ref,
    q_ref,
    local_ref,
    gate_ref,
    cotangent_ref,
    gain_ref,
    attended_ref,
    states_ref,
    sums_ref,
    unbroken_ref,
):
    place = place_ref[0]
    chip, core = place // 2, lax.rem(place, 2)
    over_slab = power(facts_ref, float(tokens))
    slabs = all_ref.shape[0]
    state = jnp.zeros((WIDTH, WIDTH), F32)
    for c in range(slabs // 2):
        before = c < chip
        factor = all_ref[2 * c, HALF : HALF + 1] * all_ref[2 * c + 1, HALF : HALF + 1]
        state = jnp.where(
            before, state * (factor * over_slab * over_slab) + chip_state(all_ref, c), state
        )
    state = jnp.where(
        core == 1,
        state * (other_ref[WIDTH : WIDTH + 1] * over_slab) + other_ref[:WIDTH],
        state,
    )
    for s in range(slabs):
        unbroken_ref[s : s + 1] = all_ref[s, HALF : HALF + 1]
    decay_in = jnp.exp(-rate_row(facts_ref) * rows_iota(BLOCK))
    over_block = power(facts_ref, float(BLOCK))
    ones = jnp.ones((8, 2 * WIDTH), BF16)
    first = lax.broadcasted_iota(jnp.int32, (8, BLOCK), 0) == 0
    for b in range(tokens // BLOCK):
        rows = block_rows(b)
        state = state * kept(facts_ref, b)
        states_ref[b] = state
        attended = local_ref[rows] + decay_in * dot_split(q_ref[rows], state)
        attended_ref[rows] = attended
        opening = jax.nn.sigmoid(gate_ref[rows].astype(F32))
        grad_norm = cotangent_ref[rows].astype(F32) * opening * gain_ref[...]
        squares = dot(ones, beside(*split(attended * attended)), 1, 1)
        crosses = dot(ones, beside(*split(grad_norm * attended)), 1, 1)
        both = jnp.where(first, squares, crosses)[:2]
        for p in range(sums_ref.shape[0]):
            sums_ref[p, :, b * BLOCK : (b + 1) * BLOCK] = both
        state = state * over_block + pairs_ref[b]


def spread_kernel(parts_ref, out_ref):
    total = parts_ref[0]
    for p in range(1, parts_ref.shape[0]):
        total = total + parts_ref[p]
    for p in range(out_ref.shape[0]):
        out_ref[p] = total


def beforehand_kernel(
    facts_ref,
    k_ref,
    v_ref,
    gate_ref,
    cotangent_ref,
    gain_ref,
    attended_ref,
    states_ref,
    query_ref,
):
    weights = decay_matrix(facts_ref)
    decay_in = jnp.exp(-rate_row(facts_ref) * rows_iota(BLOCK))
    for b in range(k_ref.shape[0] // BLOCK):
        rows = block_rows(b)
        k, v = k_ref[rows], v_ref[rows]
        opening = jax.nn.sigmoid(gate_ref[rows].astype(F32))
        grad_norm = cotangent_ref[rows].astype(F32) * opening * gain_ref[...]
        twice = beside(v, v)
        state_high, state_low = split(states_ref[b])
        state_twice = beside(state_high, state_high)
        for i, left in enumerate((grad_norm, attended_ref[rows])):
            high, low = split(left)
            both = beside(high, low)
            across = dot(both, state_twice, 1, 1) + dot(high, state_low, 1, 1)
            high, low = split(dot(both, twice, 1, 1) * weights)
            query_ref[i, rows] = dot(high, k) + dot(low, k) + decay_in * across


def thirds(row):
    high = row.astype(BF16).astype(F32)
    rest = row - high
    middle = rest.astype(BF16).astype(F32)
    return high, middle, rest - middle


def columns_of(first, second):
    pieces = thirds(first) + thirds(second)
    n = first.shape[1]
    at = lax.broadcasted_iota(jnp.int32, (16, n), 0)
    stacked = jnp.zeros((16, n), F32)
    for i, piece in enumerate(pieces):
        stacked = jnp.where(at == i, piece, stacked)
    row = lax.broadcasted_iota(jnp.int32, (16, 2 * WIDTH), 0)
    column = lax.broadcasted_iota(jnp.int32, (16, 2 * WIDTH), 1)
    chosen = jnp.where((row >= 3) == (column >= WIDTH), 1.0, 0.0).astype(BF16)
    both = dot(stacked.astype(BF16), chosen, 0, 0)
    return both[:, :WIDTH], both[:, WIDTH:]


def grad_kernel(
    features,
    row_total,
    facts_ref,
    parts_ref,
    attended_ref,
    q_ref,
    gate_ref,
    cotangent_ref,
    gain_ref,
    query_ref,
    own_ref,
    gain_part_ref,
    grad_ref,
    pieces_ref,
    mixed_ref,
    gate_grad_ref,
    query_grad_ref,
):
    total = parts_ref[0]
    for p in range(1, parts_ref.shape[0]):
        total = total + parts_ref[p]
    inverse_row = lax.rsqrt(total[0:1] * (1.0 / features) + EPSILON)
    slope_row = inverse_row * total[1:2] * (1.0 / features)
    decay_on = jnp.exp(-rate_row(facts_ref) * (rows_iota(BLOCK) + 1.0))
    over_block = power(facts_ref, float(BLOCK))
    carried = jnp.zeros((WIDTH, WIDTH), F32)
    gain_sum = jnp.zeros((1, WIDTH), F32)
    for b in reversed(range(q_ref.shape[0] // BLOCK)):
        rows = block_rows(b)
        lanes = slice(b * BLOCK, (b + 1) * BLOCK)
        inverse, slope = columns_of(inverse_row[:, lanes], slope_row[:, lanes])
        normed = attended_ref[rows] * inverse
        opening = jax.nn.sigmoid(gate_ref[rows].astype(F32))
        grad_open = cotangent_ref[rows].astype(F32) * opening
        gain_sum = gain_sum + jnp.sum(grad_open * normed, axis=0, keepdims=True)
        grad_norm = grad_open * gain_ref[...]
        grad = inverse * (grad_norm - normed * slope)
        grad_ref[rows] = beside(*split(grad))
        mixed_ref[rows] = (opening * gain_ref[...] * normed).astype(BF16)
        gate_grad_ref[rows] = (grad_norm * normed * (1.0 - opening)).astype(BF16)
        query_grad_ref[rows] = (
            inverse * (query_ref[0, rows] - inverse * slope * query_ref[1, rows])
        ).astype(BF16)
        piece = dot_split(q_ref[rows], decay_on * grad, 0)
        pieces_ref[b] = piece
        carried = (carried * over_block + piece) * kept(facts_ref, b)
    own_ref[...] = carried
    gain_part_ref[...] = gain_sum * (1.0 / math.sqrt(row_total))


def backward_kernel(
    facts_ref,
    q_ref,
    k_ref,
    v_ref,
    grad_ref,
    mixed_ref,
    gate_grad_ref,
    query_grad_ref,
    mixed_hbm,
    gate_grad_hbm,
    query_grad_hbm,
    key_part_ref,
    value_part_ref,
    sems,
):
    copies = [
        pltpu.make_async_copy(mixed_ref, mixed_hbm.at[0], sems.at[0]),
        pltpu.make_async_copy(gate_grad_ref, gate_grad_hbm.at[0], sems.at[1]),
        pltpu.make_async_copy(query_grad_ref, query_grad_hbm.at[0], sems.at[2]),
    ]
    for copy in copies:
        copy.start()
    weights = decay_matrix(facts_ref, 1)
    for b in range(q_ref.shape[0] // BLOCK):
        rows = block_rows(b)
        q, k, v, both = q_ref[rows], k_ref[rows], v_ref[rows], grad_ref[rows]
        high, low = split(dot(beside(v, v), both, 1, 1) * weights)
        key_part_ref[rows] = dot(high, q) + dot(low, q)
        high, low = split(dot(k, q, 1, 1) * weights)
        value_part_ref[rows] = halves(dot(high, both)) + dot(low, both[:, :WIDTH])
    for copy in copies:
        copy.wait()


def finish_kernel(
    tokens,
    place_ref,
    facts_ref,
    all_ref,
    other_ref,
    unbroken_ref,
    pieces_ref,
    k_ref,
    v_ref,
    key_part_ref,
    value_part_ref,
    key_grad_hbm,
    value_grad_hbm,
    gain_grad_ref,
    key_rows,
    value_rows,
    sems,
):
    copies = []
    place = place_ref[0]
    chip, core = place // 2, lax.rem(place, 2)
    over_slab = power(facts_ref, float(tokens))
    slabs = all_ref.shape[0]
    state = jnp.zeros((WIDTH, WIDTH), F32)
    for c in reversed(range(slabs // 2)):
        after = c > chip
        factor = unbroken_ref[2 * c : 2 * c + 1] * unbroken_ref[2 * c + 1 : 2 * c + 2]
        state = jnp.where(
            after, state * (factor * over_slab * over_slab) + chip_state(all_ref, c), state
        )
    partner = unbroken_ref[pl.ds(place - core + 1, 1)]
    state = jnp.where(core == 0, state * (partner * over_slab) + other_ref[...], state)
    gain = all_ref[0, HALF : HALF + 1]
    for s in range(1, slabs):
        gain = gain + all_ref[s, HALF : HALF + 1]
    gain_grad_ref[...] = gain
    decay_back = jnp.exp(-rate_row(facts_ref) * (float(BLOCK - 1) - rows_iota(BLOCK)))
    over_block = power(facts_ref, float(BLOCK))
    last = tokens // BLOCK - 1
    for b in reversed(range(last + 1)):
        rows = block_rows(b)
        if b < last:
            state = state * kept(facts_ref, b + 1)
        high, low = split(state)
        both = dot(k_ref[rows], beside(high, low))
        value_rows[rows] = (value_part_ref[rows] + decay_back * halves(both)).astype(BF16)
        both = dot(v_ref[rows], jnp.concatenate([high, low], axis=0), 1, 1)
        key_rows[rows] = (key_part_ref[rows] + decay_back * halves(both)).astype(BF16)
        for i, (source, target) in enumerate(
            ((key_rows, key_grad_hbm), (value_rows, value_grad_hbm))
        ):
            copy = pltpu.make_async_copy(
                source.at[rows], target.at[0, rows], sems.at[2 * b + i]
            )
            copy.start()
            copies.append(copy)
        state = state * over_block + pieces_ref[b]
    for copy in copies:
        copy.wait()


SMEM = pl.BlockSpec(memory_space=pltpu.SMEM)
VMEM = pl.BlockSpec(memory_space=pltpu.VMEM)
HBM = pl.BlockSpec(memory_space=pltpu.HBM)


def call(kernel, arrays, outs, flops=1 << 24, ins=None, out_specs=None, scratch=()):
    ins = ins or []
    moved = sum(math.prod(a.shape) * a.dtype.itemsize for a in (*arrays, *outs))
    return pl.pallas_call(
        kernel,
        out_shape=outs,
        in_specs=ins + [VMEM] * (len(arrays) - len(ins)),
        out_specs=out_specs or [VMEM] * len(outs),
        scratch_shapes=scratch,
        compiler_params=pltpu.CompilerParams(vmem_limit_bytes=LIMIT),
        cost_estimate=pl.CostEstimate(flops=flops, bytes_accessed=moved, transcendentals=0),
    )(*arrays)


def shape(*dims, dtype=F32):
    return jax.ShapeDtypeStruct(dims, dtype)


def bound(kernel, *fixed):
    def run(*refs):
        kernel(*fixed, *refs)

    return run


def body(queries, key_tokens, values, gate_logits, cotangent, decay_rates, norm_gain, block_starts):
    tokens = queries.shape[1]
    blocks = tokens // BLOCK
    slabs = lax.axis_size("ctx")
    outer, inner = lax.axis_size("dp"), lax.axis_size("pipe")
    features = float(WIDTH * outer * inner)
    place = lax.axis_index("ctx").astype(jnp.int32).reshape(1)
    partners = [(j, j ^ 1) for j in range(slabs)]
    whole = shape(1, tokens, WIDTH, dtype=BF16)
    like = shape(tokens, WIDTH, dtype=BF16)
    wide = shape(tokens, WIDTH)
    states = shape(blocks, WIDTH, WIDTH)
    two_wide = shape(2, tokens, WIDTH)
    dma = pltpu.SemaphoreType.DMA

    gate, cot = (a.reshape(tokens, WIDTH) for a in (gate_logits, cotangent))
    own, pairs, facts, keys, vals, quer, gain = call(
        closing_kernel,
        (
            decay_rates,
            *(
                pltpu.with_memory_space_constraint(a, pltpu.HBM)
                for a in (
                block_starts,
                key_tokens,
                values,
                queries,
                norm_gain,
                )
            ),
        ),
        [
            shape(WIDTH + 8, WIDTH),
            states,
            shape(8, BLOCK),
            like,
            like,
            like,
            shape(1, WIDTH),
        ],
        ins=[SMEM] + [HBM] * 5,
        scratch=[
            pltpu.SMEM((1, blocks), jnp.int32),
            dma((3 + 2 * blocks,)),
        ],
    )
    other = lax.ppermute(own, "ctx", partners)
    (local,) = call(local_kernel, (facts, quer, keys, vals), [wide], flops=1 << 28)
    (half,) = call(
        bound(forward_half_kernel, tokens),
        (place, facts, own, other),
        [shape(HALF + 8, WIDTH)],
        ins=[SMEM],
    )
    everyone = lax.all_gather(half, "ctx")
    attended, states_in, sums, unbroken = call(
        bound(attended_kernel, tokens),
        (place, facts, everyone, other, pairs, quer, local, gate, cot, gain),
        [wide, states, shape(inner, 2, tokens), shape(slabs, WIDTH)],
        ins=[SMEM],
    )
    sums = lax.all_to_all(sums, "pipe", 0, 0, tiled=True)
    (sums,) = call(spread_kernel, (sums,), [shape(outer, 2, tokens)])
    sums = lax.all_to_all(sums, "dp", 0, 0, tiled=True)
    (query_parts,) = call(
        beforehand_kernel,
        (facts, keys, vals, gate, cot, gain, attended, states_in),
        [shape(2, tokens, WIDTH)],
        flops=1 << 30,
    )
    back, gain_part, grad, pieces, mixed, gate_part, query_part = call(
        bound(grad_kernel, features, tokens * slabs),
        (facts, sums, attended, quer, gate, cot, gain, query_parts),
        [
            shape(WIDTH, WIDTH),
            shape(1, WIDTH),
            shape(tokens, 2 * WIDTH, dtype=BF16),
            states,
            like,
            like,
            like,
        ],
    )
    back_other = lax.ppermute(back, "ctx", partners)
    mixed_out, gate_grad, query_grad, key_part, value_part = call(
        backward_kernel,
        (facts, quer, keys, vals, grad, mixed, gate_part, query_part),
        [whole, whole, whole, wide, wide],
        out_specs=[HBM] * 3 + [VMEM] * 2,
        scratch=[dma((3,))],
        flops=1 << 30,
    )
    (back_half,) = call(
        bound(backward_half_kernel, tokens),
        (place, facts, back, back_other, gain_part, unbroken),
        [shape(HALF + 8, WIDTH)],
        ins=[SMEM],
    )
    back_everyone = lax.all_gather(back_half, "ctx")
    key_grad, value_grad, gain_grad = call(
        bound(finish_kernel, tokens),
        (
            place,
            facts,
            back_everyone,
            back_other,
            unbroken,
            pieces,
            keys,
            vals,
            key_part,
            value_part,
        ),
        [whole, whole, shape(1, WIDTH)],
        ins=[SMEM],
        out_specs=[HBM] * 2 + [VMEM],
        scratch=[
            pltpu.VMEM((tokens, WIDTH), BF16),
            pltpu.VMEM((tokens, WIDTH), BF16),
            dma((2 * blocks,)),
        ],
    )
    return (mixed_out, query_grad, key_grad, value_grad, gate_grad, gain_grad)


def solution(mesh):
    wide = P(None, "ctx", ("dp", "pipe"))
    heads = P(("dp", "pipe"))
    gain = P(("dp", "pipe"), None)
    return jax.shard_map(
        body,
        mesh=mesh,
        in_specs=(wide, wide, wide, wide, wide, heads, gain, P(None, "ctx")),
        out_specs=(wide, wide, wide, wide, wide, gain),
        check_vma=False,
    )
```

time: 99.7 us -> 95.3 us (0.956)
  blocking collectives: 61.4 us -> 39.3 us
  starting transfers between devices: 21.9 us -> 32.6 us
  waiting for transfers between devices: 0.01 us -> 9.83 us
  local copies, waits for them, and re-layouts: 3.51 us -> 0.01 us
    all_to_all x1 -> x0, blocking collectives: 22.2 us -> none  [body(): sums = lax.all_to_all(sums, 'dp', 0, 0, tiled=True)]
    all_to_all x0 -> x1, starting transfers between devices: none -> 10.7 us  [body(): sums = lax.all_to_all(sums, 'dp', 0, 0, tiled=True)]
    all_to_all x0 -> x1, waiting for transfers between devices: none -> 9.83 us  [body(): sums = lax.all_to_all(sums, 'dp', 0, 0, tiled=True)]
    unnamed x20 -> x4, local copies, waits for them, and re-layouts: 3.51 us -> 0.01 us
    pallas_call x9 -> x10, Pallas kernels: 11 us -> 11.8 us  [call(): pl.pallas_call(kernel, out_shape=outs, in_specs=ins + [VMEM] * (len(array...]
  transfers between devices with their start and end apart: 2 -> 3, of which waited for: 0 -> 1; matrix products, arithmetic and copies ran while one was open for 0% -> 0% of each run, Pallas kernels for 5% -> 6%
where the time goes in v2:
time: 95.3 us; the launch traced here: 94.9 us
  blocking collectives  39.3 us (41%)
  starting transfers between devices  32.6 us (34%)
  Pallas kernels  11.8 us (12%)
  waiting for transfers between devices  9.83 us (10%)
  between operations  1.39 us (1%)
    all_gather x1, blocking collectives, body(): back_everyone = lax.all_gather(back_half, 'ctx')  16.4 us
    all_gather x1, blocking collectives, body(): everyone = lax.all_gather(half, 'ctx')  16.2 us
    ppermute x1, starting transfers between devices, body(): other = lax.ppermute(own, 'ctx', partners)  16 us
    pallas_call x10, Pallas kernels, call(): pl.pallas_call(kernel, out_shape=outs, in_specs=ins + [VMEM] * (len(array...  11.8 us
    all_to_all x1, starting transfers between devices, body(): sums = lax.all_to_all(sums, 'dp', 0, 0, tiled=True)  10.7 us
    all_to_all x1, waiting for transfers between devices, body(): sums = lax.all_to_all(sums, 'dp', 0, 0, tiled=True)  9.83 us
    all_to_all x1, blocking collectives, body(): sums = lax.all_to_all(sums, 'pipe', 0, 0, tiled=True)  6.65 us
    ppermute x1, starting transfers between devices, body(): back_other = lax.ppermute(back, 'ctx', partners)  5.92 us
  transfers between devices with their start and end apart: 3, of which 1 were waited for; matrix products, arithmetic and copies ran while one was open for 0% of the time, Pallas kernels for 6%

profile of v2, /device:TPU:1, one launch (start us, length us, event | category | flops | bytes accessed | tf_op | source)
XLA Modules:
  0.0 94.9 jit_solution(9440161597426314648)
XLA Ops:
  1.3 1.8 %shard_map.127 = (f32[136,128]{1,0:T(8,128)S(1)}, f32[4,128,128]{2,1,0:T(8,128)S(1)}, f32[8,256]{1,0:T(8,128)S(1)}, bf16[1024,128]{1,0:T(8,128)(2,1)S(1)}, bf16[...) custom-call(f32[1]{0:T(128)S(6)} %copy.14.rate_ref, s32[1,4]{1,0:T(1,128)} %flags_hbm.1, ...), custom_call_target="tpu_custom_call" | custom-call | flops 16777216 | bytes 1913876 | tf_op jit(solution)/shard_map/pallas_call | solution.py:443
  3.1 16.0 %collective-permute-start = (f32[136,128]{1,0:T(8,128)S(1)}, f32[136,128]{1,0:T(8,128)S(1)}, u32[]{:S(2)}, u32[]{:S(2)}) collective-permute-start(f32[136,128]{1,0:T(8,128)S(1)} %get-tuple-element.36.refs_2_), channel_id=1, source_target_pairs={{0,64},{64,0},{128,192},{192,128},{256,320},{320,256},{384,448},{4... | collective-permute-start | bytes 208904 | tf_op jit(solution)/shard_map/ppermute | solution.py:511
  19.1 0.9 shard_map.129.refs_6_
  20.0 0.0 collective-permute-done.refs_3_
  20.1 0.0 copy-start
  20.1 0.0 copy-start.1
  20.1 16.2 %all-gather = f32[1152,128]{1,0:T(8,128)S(1)} all-gather(f32[72,128]{1,0:T(8,128)S(1)} %shard_map.128), channel_id=2, replica_groups=mesh['ctx'=16,'dp'=16,'pipe'=4] {'ctx'}, dimensions={0}, use_global_device_ids=true | all-gather | bytes 626688 | tf_op jit(solution)/shard_map/all_gather | solution.py:519
  36.3 0.0 copy-done
  36.3 0.0 copy-done.1
  36.3 1.0 %shard_map.130 = (f32[1024,128]{1,0:T(8,128)S(1)}, f32[4,128,128]{2,1,0:T(8,128)S(1)}, f32[4,2,1024]{2,1,0:T(2,128)S(1)}, f32[16,128]{1,0:T(8,128)S(1)}) custom-call(s32[1]{0:T(128)} %bitcast.refs_0_, f32[8,256]{1,0:T(8,128)S(1)} %get-tuple-element.32.refs_1_.facts_ref.refs_0_, f32[16,72,128]{2,1,0:T(8,128)S(1)} %bitcast.6, ...), custom_call_target="tpu_custom_call" | custom-call | flops 16777216 | bytes 3068420 | tf_op jit(solution)/shard_map/pallas_call | solution.py:443
  37.4 6.7 %all_to_all.10.parts_ref = f32[4,2,1024]{2,1,0:T(2,128)S(1)} all-to-all(f32[4,2,1024]{2,1,0:T(2,128)S(1)} %get-tuple-element.39), channel_id=1, replica_groups=mesh['ctx'=16,'dp'=16,'pipe'=4] {'pipe'}, dimensions={0} | all-to-all | bytes 65536 | tf_op jit(solution)/shard_map/all_to_all | solution.py:526
  44.0 0.7 shard_map.131
  44.7 10.7 %all-to-all-start.1 = ((f32[16,2,1024]{2,1,0:T(2,128)}), f32[16,2,1024]{2,1,0:T(2,128)S(1)}, u32[]{:S(2)}, u32[]{:S(2)}) async-start(f32[16,2,1024]{2,1,0:T(2,128)} %shard_map.131), calls=%async_computation.1 | async-start | bytes 262144 | tf_op jit(solution)/shard_map/all_to_all | solution.py:528
  55.4 2.1 %shard_map.132.refs_7_ = f32[2,1024,128]{2,1,0:T(8,128)S(1)} custom-call(f32[8,256]{1,0:T(8,128)S(1)} %get-tuple-element.32.refs_1_.facts_ref.refs_0_, bf16[1024,128]{1,0:T(8,128)(2,1)S(1)} %get-tuple-element.34.k_ref.refs_6_, bf16[1024,128]{1,0:T(8,128)(2,1)S(1)} %get-tuple-element.35.v_ref.refs_7_, bf16[1024,128]{1,0:T(8,128)(2,1)S(1)} %bitcast.8, ...), custom_call_target="tpu_custom_call" | custom-call | flops 1073741824 | bytes 2892288 | tf_op jit(solution)/shard_map/pallas_call | solution.py:443
  57.5 9.8 %all-to-all-done.1.refs_1_ = f32[16,2,1024]{2,1,0:T(2,128)S(1)} async-done(((f32[16,2,1024]{2,1,0:T(2,128)}), f32[16,2,1024]{2,1,0:T(2,128)S(1)}, u32[]{:S(2)}, u32[]{:S(2)}) %all-to-all-start.1) | async-done | bytes 131104 | tf_op jit(solution)/shard_map/all_to_all | solution.py:528
  67.3 1.3 %shard_map.133 = (f32[128,128]{1,0:T(8,128)S(1)}, f32[1,128]{1,0:T(1,128)S(1)}, bf16[1024,256]{1,0:T(8,128)(2,1)S(1)}, f32[4,128,128]{2,1,0:T(8,128)S(1)}, bf16[...) custom-call(f32[8,256]{1,0:T(8,128)S(1)} %get-tuple-element.32.refs_1_.facts_ref.refs_0_, ...), custom_call_target="tpu_custom_call" | custom-call | flops 16777216 | bytes 4137984 | tf_op jit(solution)/shard_map/pallas_call | solution.py:443
  68.6 5.9 %collective-permute-start.1 = (f32[128,128]{1,0:T(8,128)S(1)}, f32[128,128]{1,0:T(8,128)S(1)}, u32[]{:S(2)}, u32[]{:S(2)}) collective-permute-start(f32[128,128]{1,0:T(8,128)S(1)} %get-tuple-element.48.refs_2_), channel_id=1, source_target_pairs={{0,64},{64,0},{128,192},{192,128},{256,320},{320,256},{384,448},{4... | collective-permute-start | bytes 196616 | tf_op jit(solution)/shard_map/ppermute | solution.py:548
  74.6 2.2 %shard_map.134 = (bf16[1,1024,128]{2,1,0:T(8,128)(2,1)}, bf16[1,1024,128]{2,1,0:T(8,128)(2,1)}, bf16[1,1024,128]{2,1,0:T(8,128)(2,1)}, f32[1024,128]{1,0:T(8,128)S(1)}, f32[1024,128]{1,0:T(8,128)S(1)}) custom-call(f32[8,256]{1,0:T(8,128)S(1)} %get-tuple-element.32.refs_1_.facts_ref.refs_0_, bf16[1024,128]{1,0:T(8,128)(2,1)S(1)} %get-tuple-element.33.q_ref.refs_5_.refs_3_, ...), custom_call_target="tpu_custom_call" | custom-call | flops 1073741824 | bytes 3940352 | tf_op jit(solution)/shard_map/pallas_call | solution.py:443
  76.7 0.0 collective-permute-done.1.refs_3_
  76.8 16.4 %all-gather.1 = f32[1152,128]{1,0:T(8,128)S(1)} all-gather(f32[72,128]{1,0:T(8,128)S(1)} %shard_map.135), channel_id=3, replica_groups=mesh['ctx'=16,'dp'=16,'pipe'=4] {'ctx'}, dimensions={0}, use_global_device_ids=true | all-gather | bytes 626688 | tf_op jit(solution)/shard_map/all_gather | solution.py:563
  93.2 1.8 %shard_map.136 = (bf16[1,1024,128]{2,1,0:T(8,128)(2,1)}, bf16[1,1024,128]{2,1,0:T(8,128)(2,1)}, f32[1,128]{1,0:T(1,128)}) custom-call(s32[1]{0:T(128)} %bitcast.refs_0_, f32[8,256]{1,0:T(8,128)S(1)} %get-tuple-element.32.refs_1_.facts_ref.refs_0_, f32[16,72,128]{2,1,0:T(8,128)S(1)} %bitcast.5, f32[128,128]{1,0:T(8,128)S(1)} %collective-permute-done.1.refs_3_, ...), custom_call_target="tpu_custom_call" | custom-call | flops 16777216 | bytes 3031556 | tf_op jit(solution)/shard_map/pallas_call | solution.py:443
  (2 shorter events, 0.0 us)
Async XLA Ops:
  3.1 17.0 %collective-permute-start = (f32[136,128]{1,0:T(8,128)S(1)}, f32[136,128]{1,0:T(8,128)S(1)}, u32[]{:S(2)}, u32[]{:S(2)}) collective-permute-start(f32[136,128]{1,0:T(8,128)S(1)} %get-tuple-element.36.refs_2_), channel_id=1, source_target_pairs={{0,64},{64,0},{128,192},{192,128},{256,320},{320,256},{384,448},{4... | collective-permute-start | bytes 208904 | tf_op jit(solution)/shard_map/ppermute | solution.py:511
  20.1 16.2 %copy-start = (bf16[1,1024,128]{2,1,0:T(8,128)(2,1)S(1)}, bf16[1,1024,128]{2,1,0:T(8,128)(2,1)}, u32[]{:S(2)}) copy-start(bf16[1,1024,128]{2,1,0:T(8,128)(2,1)} %param.11) | copy-start | bytes 786436
  20.1 16.2 %copy-start.1 = (bf16[1,1024,128]{2,1,0:T(8,128)(2,1)S(1)}, bf16[1,1024,128]{2,1,0:T(8,128)(2,1)}, u32[]{:S(2)}) copy-start(bf16[1,1024,128]{2,1,0:T(8,128)(2,1)} %param.12) | copy-start | bytes 786436
  44.7 22.6 %all-to-all-start.1 = ((f32[16,2,1024]{2,1,0:T(2,128)}), f32[16,2,1024]{2,1,0:T(2,128)S(1)}, u32[]{:S(2)}, u32[]{:S(2)}) async-start(f32[16,2,1024]{2,1,0:T(2,128)} %shard_map.131), calls=%async_computation.1 | async-start | bytes 262144 | tf_op jit(solution)/shard_map/all_to_all | solution.py:528
  68.6 8.1 %collective-permute-start.1 = (f32[128,128]{1,0:T(8,128)S(1)}, f32[128,128]{1,0:T(8,128)S(1)}, u32[]{:S(2)}, u32[]{:S(2)}) collective-permute-start(f32[128,128]{1,0:T(8,128)S(1)} %get-tuple-element.48.refs_2_), channel_id=1, source_target_pairs={{0,64},{64,0},{128,192},{192,128},{256,320},{320,256},{384,448},{4... | collective-permute-start | bytes 196616 | tf_op jit(solution)/shard_map/ppermute | solution.py:548

commit v3 on v2

--- a/solution.py
+++ b/solution.py
@@ -107,23 +107,23 @@
     ]
     for copy in rest:
         copy.start()
+    facts_ref[0:1] = jnp.full((1, BLOCK), rate_ref[0], F32)
+    rate = jnp.full((1, WIDTH), rate_ref[0], F32)
+    decay_out = jnp.exp(-rate * (float(BLOCK) - rows_iota(BLOCK)))
+    over_block = jnp.exp(-rate * float(BLOCK))
+    for b in range(blocks):
+        for copy in parts[b]:
+            copy.wait()
+        rows = block_rows(b)
+        pairs_ref[b] = dot_split(k_ref[rows], decay_out * v_ref[rows].astype(F32), 0)
     flags_copy.wait()
-    facts_ref[0:1] = jnp.full((1, BLOCK), rate_ref[0], F32)
     unbroken = 1.0
+    carried = jnp.zeros((WIDTH, WIDTH), F32)
     for b in range(blocks):
         keep = 1.0 - flags_smem[0, b].astype(F32)
         unbroken = unbroken * keep
         facts_ref[b + 1 : b + 2] = jnp.full((1, BLOCK), keep, F32)
-    decay_out = jnp.exp(-rate_row(facts_ref) * (float(BLOCK) - rows_iota(BLOCK)))
-    over_block = power(facts_ref, float(BLOCK))
-    carried = jnp.zeros((WIDTH, WIDTH), F32)
-    for b in range(blocks):
-        for copy in parts[b]:
-            copy.wait()
-        rows = block_rows(b)
-        piece = dot_split(k_ref[rows], decay_out * v_ref[rows].astype(F32), 0)
-        pairs_ref[b] = piece
-        carried = carried * (over_block * kept(facts_ref, b)) + piece
+        carried = carried * (over_block * keep) + pairs_ref[b]
     own_ref[:WIDTH] = carried
     own_ref[WIDTH:] = jnp.full((8, WIDTH), unbroken, F32)
     for copy in rest:
@@ -132,12 +132,20 @@
 
 def local_kernel(facts_ref, q_ref, k_ref, v_ref, out_ref):
     weights = decay_matrix(facts_ref)
-    for b in range(q_ref.shape[0] // BLOCK):
-        rows = block_rows(b)
-        scores = dot(q_ref[rows], k_ref[rows], 1, 1) * weights
-        high, low = split(scores)
-        v = v_ref[rows]
-        out_ref[rows] = dot(high, v) + dot(low, v)
+    blocks = q_ref.shape[0] // BLOCK
+    ahead = None
+    for b in range(blocks + 1):
+        coming = None
+        if b < blocks:
+            rows = block_rows(b)
+            scores = dot(q_ref[rows], k_ref[rows], 1, 1)
+        if ahead is not None:
+            before = block_rows(b - 1)
+            v = v_ref[before]
+            out_ref[before] = dot(ahead[0], v) + dot(ahead[1], v)
+        if b < blocks:
+            coming = split(scores * weights)
+        ahead = coming
 
 
 def forward_half_kernel(tokens, place_ref, facts_ref, own_ref, other_ref, out_ref):
@@ -210,20 +218,32 @@
     over_block = power(facts_ref, float(BLOCK))
     ones = jnp.ones((8, 2 * WIDTH), BF16)
     first = lax.broadcasted_iota(jnp.int32, (8, BLOCK), 0) == 0
-    for b in range(tokens // BLOCK):
-        rows = block_rows(b)
+    blocks = tokens // BLOCK
+    for b in range(blocks):
         state = state * kept(facts_ref, b)
         states_ref[b] = state
-        attended = local_ref[rows] + decay_in * dot_split(q_ref[rows], state)
-        attended_ref[rows] = attended
-        opening = jax.nn.sigmoid(gate_ref[rows].astype(F32))
-        grad_norm = cotangent_ref[rows].astype(F32) * opening * gain_ref[...]
-        squares = dot(ones, beside(*split(attended * attended)), 1, 1)
-        crosses = dot(ones, beside(*split(grad_norm * attended)), 1, 1)
-        both = jnp.where(first, squares, crosses)[:2]
-        for p in range(sums_ref.shape[0]):
-            sums_ref[p, :, b * BLOCK : (b + 1) * BLOCK] = both
         state = state * over_block + pairs_ref[b]
+
+    def across(b):
+        high, low = split(states_ref[b])
+        return dot(q_ref[block_rows(b)], beside(high, low))
+
+    ahead, behind = across(0), None
+    for b in range(blocks + 1):
+        coming = across(b + 1) if b + 1 < blocks else None
+        if b < blocks:
+            rows = block_rows(b)
+            attended = local_ref[rows] + decay_in * halves(ahead)
+            attended_ref[rows] = attended
+            opening = jax.nn.sigmoid(gate_ref[rows].astype(F32))
+            grad_norm = cotangent_ref[rows].astype(F32) * opening * gain_ref[...]
+            squares = dot(ones, beside(*split(attended * attended)), 1, 1)
+            crosses = dot(ones, beside(*split(grad_norm * attended)), 1, 1)
+        if behind is not None:
+            both = jnp.where(first, *behind)[:2]
+            for p in range(sums_ref.shape[0]):
+                sums_ref[p, :, (b - 1) * BLOCK : b * BLOCK] = both
+        ahead, behind = coming, (squares, crosses)
 
 
 def spread_kernel(parts_ref, out_ref):
@@ -312,25 +332,36 @@
     over_block = power(facts_ref, float(BLOCK))
     carried = jnp.zeros((WIDTH, WIDTH), F32)
     gain_sum = jnp.zeros((1, WIDTH), F32)
-    for b in reversed(range(q_ref.shape[0] // BLOCK)):
-        rows = block_rows(b)
+    blocks = q_ref.shape[0] // BLOCK
+
+    def columns(b):
         lanes = slice(b * BLOCK, (b + 1) * BLOCK)
-        inverse, slope = columns_of(inverse_row[:, lanes], slope_row[:, lanes])
-        normed = attended_ref[rows] * inverse
-        opening = jax.nn.sigmoid(gate_ref[rows].astype(F32))
-        grad_open = cotangent_ref[rows].astype(F32) * opening
-        gain_sum = gain_sum + jnp.sum(grad_open * normed, axis=0, keepdims=True)
-        grad_norm = grad_open * gain_ref[...]
-        grad = inverse * (grad_norm - normed * slope)
-        grad_ref[rows] = beside(*split(grad))
-        mixed_ref[rows] = (opening * gain_ref[...] * normed).astype(BF16)
-        gate_grad_ref[rows] = (grad_norm * normed * (1.0 - opening)).astype(BF16)
-        query_grad_ref[rows] = (
-            inverse * (query_ref[0, rows] - inverse * slope * query_ref[1, rows])
-        ).astype(BF16)
-        piece = dot_split(q_ref[rows], decay_on * grad, 0)
-        pieces_ref[b] = piece
-        carried = (carried * over_block + piece) * kept(facts_ref, b)
+        return columns_of(inverse_row[:, lanes], slope_row[:, lanes])
+
+    ahead, behind = columns(blocks - 1), None
+    for b in reversed(range(-1, blocks)):
+        coming = columns(b - 1) if b > 0 else None
+        piece = None
+        if b >= 0:
+            rows = block_rows(b)
+            inverse, slope = ahead
+            normed = attended_ref[rows] * inverse
+            opening = jax.nn.sigmoid(gate_ref[rows].astype(F32))
+            grad_open = cotangent_ref[rows].astype(F32) * opening
+            gain_sum = gain_sum + jnp.sum(grad_open * normed, axis=0, keepdims=True)
+            grad_norm = grad_open * gain_ref[...]
+            grad = inverse * (grad_norm - normed * slope)
+            piece = dot_split(q_ref[rows], decay_on * grad, 0)
+            grad_ref[rows] = beside(*split(grad))
+            mixed_ref[rows] = (opening * gain_ref[...] * normed).astype(BF16)
+            gate_grad_ref[rows] = (grad_norm * normed * (1.0 - opening)).astype(BF16)
+            query_grad_ref[rows] = (
+                inverse * (query_ref[0, rows] - inverse * slope * query_ref[1, rows])
+            ).astype(BF16)
+        if behind is not None:
+            pieces_ref[b + 1] = behind
+            carried = (carried * over_block + behind) * kept(facts_ref, b + 1)
+        ahead, behind = coming, piece
     own_ref[...] = carried
     gain_part_ref[...] = gain_sum * (1.0 / math.sqrt(row_total))
 
@@ -359,13 +390,26 @@
     for copy in copies:
         copy.start()
     weights = decay_matrix(facts_ref, 1)
-    for b in range(q_ref.shape[0] // BLOCK):
-        rows = block_rows(b)
-        q, k, v, both = q_ref[rows], k_ref[rows], v_ref[rows], grad_ref[rows]
-        high, low = split(dot(beside(v, v), both, 1, 1) * weights)
-        key_part_ref[rows] = dot(high, q) + dot(low, q)
-        high, low = split(dot(k, q, 1, 1) * weights)
-        value_part_ref[rows] = halves(dot(high, both)) + dot(low, both[:, :WIDTH])
+    blocks = q_ref.shape[0] // BLOCK
+    ahead = None
+    for b in range(blocks + 1):
+        coming = None
+        if b < blocks:
+            rows = block_rows(b)
+            v = v_ref[rows]
+            slopes = dot(beside(v, v), grad_ref[rows], 1, 1)
+            scores = dot(k_ref[rows], q_ref[rows], 1, 1)
+        if ahead is not None:
+            (slopes_high, slopes_low), (scores_high, scores_low) = ahead
+            before = block_rows(b - 1)
+            q, both = q_ref[before], grad_ref[before]
+            key_part_ref[before] = dot(slopes_high, q) + dot(slopes_low, q)
+            value_part_ref[before] = halves(dot(scores_high, both)) + dot(
+                scores_low, both[:, :WIDTH]
+            )
+        if b < blocks:
+            coming = split(slopes * weights), split(scores * weights)
+        ahead = coming
     for copy in copies:
         copy.wait()
 

time: 95.3 us -> 93.7 us (0.983)
  Pallas kernels: 11.8 us -> 9.82 us
    pallas_call x10, Pallas kernels: 11.8 us -> 9.82 us  [call(): pl.pallas_call(kernel, out_shape=outs, in_specs=ins + [VMEM] * (len(array...]
  transfers between devices with their start and end apart: 3 -> 3, of which waited for: 1 -> 2; matrix products, arithmetic and copies ran while one was open for 0% -> 0% of each run, Pallas kernels for 6% -> 4%
where the time goes in v3:
time: 93.7 us; the launch traced here: 93.3 us
  blocking collectives  39.4 us (42%)
  starting transfers between devices  32.6 us (35%)
  waiting for transfers between devices  10.1 us (11%)
  Pallas kernels  9.82 us (10%)
  between operations  1.38 us (1%)
    all_gather x1, blocking collectives, body(): back_everyone = lax.all_gather(back_half, 'ctx')  16.5 us
    all_gather x1, blocking collectives, body(): everyone = lax.all_gather(half, 'ctx')  16.3 us
    ppermute x1, starting transfers between devices, body(): other = lax.ppermute(own, 'ctx', partners)  16 us
    all_to_all x1, starting transfers between devices, body(): sums = lax.all_to_all(sums, 'dp', 0, 0, tiled=True)  10.7 us
    all_to_all x1, waiting for transfers between devices, body(): sums = lax.all_to_all(sums, 'dp', 0, 0, tiled=True)  9.83 us
    pallas_call x10, Pallas kernels, call(): pl.pallas_call(kernel, out_shape=outs, in_specs=ins + [VMEM] * (len(array...  9.82 us
    all_to_all x1, blocking collectives, body(): sums = lax.all_to_all(sums, 'pipe', 0, 0, tiled=True)  6.65 us
    ppermute x1, starting transfers between devices, body(): back_other = lax.ppermute(back, 'ctx', partners)  5.93 us
  transfers between devices with their start and end apart: 3, of which 2 were waited for; matrix products, arithmetic and copies ran while one was open for 0% of the time, Pallas kernels for 4%

profile of v3, /device:TPU:1, one launch (start us, length us, event | category | flops | bytes accessed | tf_op | source)
XLA Modules:
  0.0 93.3 jit_solution(14235622724254488425)
XLA Ops:
  1.3 1.8 %shard_map.127 = (f32[136,128]{1,0:T(8,128)S(1)}, f32[4,128,128]{2,1,0:T(8,128)S(1)}, f32[8,256]{1,0:T(8,128)S(1)}, bf16[1024,128]{1,0:T(8,128)(2,1)S(1)}, bf16[...) custom-call(f32[1]{0:T(128)S(6)} %copy.14.rate_ref, s32[1,4]{1,0:T(1,128)} %flags_hbm.1, ...), custom_call_target="tpu_custom_call" | custom-call | flops 16777216 | bytes 1913876 | tf_op jit(solution)/shard_map/pallas_call | solution.py:487
  3.1 16.0 %collective-permute-start = (f32[136,128]{1,0:T(8,128)S(1)}, f32[136,128]{1,0:T(8,128)S(1)}, u32[]{:S(2)}, u32[]{:S(2)}) collective-permute-start(f32[136,128]{1,0:T(8,128)S(1)} %get-tuple-element.36.refs_2_), channel_id=1, source_target_pairs={{0,64},{64,0},{128,192},{192,128},{256,320},{320,256},{384,448},{4... | collective-permute-start | bytes 208904 | tf_op jit(solution)/shard_map/ppermute | solution.py:555
  19.2 0.6 shard_map.129.refs_6_
  19.8 0.2 collective-permute-done.refs_3_
  20.1 0.0 copy-start
  20.1 0.0 copy-start.1
  20.1 16.3 %all-gather = f32[1152,128]{1,0:T(8,128)S(1)} all-gather(f32[72,128]{1,0:T(8,128)S(1)} %shard_map.128), channel_id=2, replica_groups=mesh['ctx'=16,'dp'=16,'pipe'=4] {'ctx'}, dimensions={0}, use_global_device_ids=true | all-gather | bytes 626688 | tf_op jit(solution)/shard_map/all_gather | solution.py:563
  36.4 0.0 copy-done
  36.4 0.0 copy-done.1
  36.4 0.7 shard_map.130
  37.1 6.7 %all_to_all.10.parts_ref = f32[4,2,1024]{2,1,0:T(2,128)S(1)} all-to-all(f32[4,2,1024]{2,1,0:T(2,128)S(1)} %get-tuple-element.39), channel_id=1, replica_groups=mesh['ctx'=16,'dp'=16,'pipe'=4] {'pipe'}, dimensions={0} | all-to-all | bytes 65536 | tf_op jit(solution)/shard_map/all_to_all | solution.py:570
  43.7 0.7 shard_map.131
  44.4 10.7 %all-to-all-start.1 = ((f32[16,2,1024]{2,1,0:T(2,128)}), f32[16,2,1024]{2,1,0:T(2,128)S(1)}, u32[]{:S(2)}, u32[]{:S(2)}) async-start(f32[16,2,1024]{2,1,0:T(2,128)} %shard_map.131), calls=%async_computation.1 | async-start | bytes 262144 | tf_op jit(solution)/shard_map/all_to_all | solution.py:572
  55.1 2.1 %shard_map.132.refs_7_ = f32[2,1024,128]{2,1,0:T(8,128)S(1)} custom-call(f32[8,256]{1,0:T(8,128)S(1)} %get-tuple-element.32.refs_1_.facts_ref.refs_0_, bf16[1024,128]{1,0:T(8,128)(2,1)S(1)} %get-tuple-element.34.k_ref.refs_6_, bf16[1024,128]{1,0:T(8,128)(2,1)S(1)} %get-tuple-element.35.v_ref.refs_7_, bf16[1024,128]{1,0:T(8,128)(2,1)S(1)} %bitcast.8, ...), custom_call_target="tpu_custom_call" | custom-call | flops 1073741824 | bytes 2892288 | tf_op jit(solution)/shard_map/pallas_call | solution.py:487
  57.2 9.8 %all-to-all-done.1.refs_1_ = f32[16,2,1024]{2,1,0:T(2,128)S(1)} async-done(((f32[16,2,1024]{2,1,0:T(2,128)}), f32[16,2,1024]{2,1,0:T(2,128)S(1)}, u32[]{:S(2)}, u32[]{:S(2)}) %all-to-all-start.1) | async-done | bytes 131104 | tf_op jit(solution)/shard_map/all_to_all | solution.py:572
  67.0 1.0 %shard_map.133 = (f32[128,128]{1,0:T(8,128)S(1)}, f32[1,128]{1,0:T(1,128)S(1)}, bf16[1024,256]{1,0:T(8,128)(2,1)S(1)}, f32[4,128,128]{2,1,0:T(8,128)S(1)}, bf16[...) custom-call(f32[8,256]{1,0:T(8,128)S(1)} %get-tuple-element.32.refs_1_.facts_ref.refs_0_, ...), custom_call_target="tpu_custom_call" | custom-call | flops 16777216 | bytes 4137984 | tf_op jit(solution)/shard_map/pallas_call | solution.py:487
  68.0 5.9 %collective-permute-start.1 = (f32[128,128]{1,0:T(8,128)S(1)}, f32[128,128]{1,0:T(8,128)S(1)}, u32[]{:S(2)}, u32[]{:S(2)}) collective-permute-start(f32[128,128]{1,0:T(8,128)S(1)} %get-tuple-element.48.refs_2_), channel_id=1, source_target_pairs={{0,64},{64,0},{128,192},{192,128},{256,320},{320,256},{384,448},{4... | collective-permute-start | bytes 196616 | tf_op jit(solution)/shard_map/ppermute | solution.py:592
  73.9 1.1 %shard_map.134 = (bf16[1,1024,128]{2,1,0:T(8,128)(2,1)}, bf16[1,1024,128]{2,1,0:T(8,128)(2,1)}, bf16[1,1024,128]{2,1,0:T(8,128)(2,1)}, f32[1024,128]{1,0:T(8,128)S(1)}, f32[1024,128]{1,0:T(8,128)S(1)}) custom-call(f32[8,256]{1,0:T(8,128)S(1)} %get-tuple-element.32.refs_1_.facts_ref.refs_0_, bf16[1024,128]{1,0:T(8,128)(2,1)S(1)} %get-tuple-element.33.q_ref.refs_5_.refs_3_, ...), custom_call_target="tpu_custom_call" | custom-call | flops 1073741824 | bytes 3940352 | tf_op jit(solution)/shard_map/pallas_call | solution.py:487
  75.0 0.0 collective-permute-done.1.refs_3_
  75.1 16.5 %all-gather.1 = f32[1152,128]{1,0:T(8,128)S(1)} all-gather(f32[72,128]{1,0:T(8,128)S(1)} %shard_map.135), channel_id=3, replica_groups=mesh['ctx'=16,'dp'=16,'pipe'=4] {'ctx'}, dimensions={0}, use_global_device_ids=true | all-gather | bytes 626688 | tf_op jit(solution)/shard_map/all_gather | solution.py:607
  91.6 1.8 %shard_map.136 = (bf16[1,1024,128]{2,1,0:T(8,128)(2,1)}, bf16[1,1024,128]{2,1,0:T(8,128)(2,1)}, f32[1,128]{1,0:T(1,128)}) custom-call(s32[1]{0:T(128)} %bitcast.refs_0_, f32[8,256]{1,0:T(8,128)S(1)} %get-tuple-element.32.refs_1_.facts_ref.refs_0_, f32[16,72,128]{2,1,0:T(8,128)S(1)} %bitcast.5, f32[128,128]{1,0:T(8,128)S(1)} %collective-permute-done.1.refs_3_, ...), custom_call_target="tpu_custom_call" | custom-call | flops 16777216 | bytes 3031556 | tf_op jit(solution)/shard_map/pallas_call | solution.py:487
  (2 shorter events, 0.0 us)
Async XLA Ops:
  3.1 16.9 %collective-permute-start = (f32[136,128]{1,0:T(8,128)S(1)}, f32[136,128]{1,0:T(8,128)S(1)}, u32[]{:S(2)}, u32[]{:S(2)}) collective-permute-start(f32[136,128]{1,0:T(8,128)S(1)} %get-tuple-element.36.refs_2_), channel_id=1, source_target_pairs={{0,64},{64,0},{128,192},{192,128},{256,320},{320,256},{384,448},{4... | collective-permute-start | bytes 208904 | tf_op jit(solution)/shard_map/ppermute | solution.py:555
  20.1 16.3 %copy-start = (bf16[1,1024,128]{2,1,0:T(8,128)(2,1)S(1)}, bf16[1,1024,128]{2,1,0:T(8,128)(2,1)}, u32[]{:S(2)}) copy-start(bf16[1,1024,128]{2,1,0:T(8,128)(2,1)} %param.11) | copy-start | bytes 786436
  20.1 16.3 %copy-start.1 = (bf16[1,1024,128]{2,1,0:T(8,128)(2,1)S(1)}, bf16[1,1024,128]{2,1,0:T(8,128)(2,1)}, u32[]{:S(2)}) copy-start(bf16[1,1024,128]{2,1,0:T(8,128)(2,1)} %param.12) | copy-start | bytes 786436
  44.4 22.6 %all-to-all-start.1 = ((f32[16,2,1024]{2,1,0:T(2,128)}), f32[16,2,1024]{2,1,0:T(2,128)S(1)}, u32[]{:S(2)}, u32[]{:S(2)}) async-start(f32[16,2,1024]{2,1,0:T(2,128)} %shard_map.131), calls=%async_computation.1 | async-start | bytes 262144 | tf_op jit(solution)/shard_map/all_to_all | solution.py:572
  68.0 7.0 %collective-permute-start.1 = (f32[128,128]{1,0:T(8,128)S(1)}, f32[128,128]{1,0:T(8,128)S(1)}, u32[]{:S(2)}, u32[]{:S(2)}) collective-permute-start(f32[128,128]{1,0:T(8,128)S(1)} %get-tuple-element.48.refs_2_), channel_id=1, source_target_pairs={{0,64},{64,0},{128,192},{192,128},{256,320},{320,256},{384,448},{4... | collective-permute-start | bytes 196616 | tf_op jit(solution)/shard_map/ppermute | solution.py:592

commit v4 on v3

--- a/solution.py
+++ b/solution.py
@@ -89,21 +89,15 @@
     blocks = k_ref.shape[0] // BLOCK
     flags_copy = pltpu.make_async_copy(flags_hbm, flags_smem, sems.at[0])
     flags_copy.start()
-    parts = []
-    for b in range(blocks):
-        rows = block_rows(b)
-        parts.append(
-            [
-                pltpu.make_async_copy(k_hbm.at[0, rows], k_ref.at[rows], sems.at[1 + 2 * b]),
-                pltpu.make_async_copy(v_hbm.at[0, rows], v_ref.at[rows], sems.at[2 + 2 * b]),
-            ]
-        )
-        for copy in parts[b]:
-            copy.start()
-    at = 1 + 2 * blocks
+    parts = [
+        pltpu.make_async_copy(k_hbm.at[0], k_ref, sems.at[1]),
+        pltpu.make_async_copy(v_hbm.at[0], v_ref, sems.at[2]),
+    ]
+    for copy in parts:
+        copy.start()
     rest = [
-        pltpu.make_async_copy(q_hbm.at[0], q_ref, sems.at[at]),
-        pltpu.make_async_copy(gain_hbm, gain_ref, sems.at[at + 1]),
+        pltpu.make_async_copy(q_hbm.at[0], q_ref, sems.at[3]),
+        pltpu.make_async_copy(gain_hbm, gain_ref, sems.at[4]),
     ]
     for copy in rest:
         copy.start()
@@ -111,19 +105,21 @@
     rate = jnp.full((1, WIDTH), rate_ref[0], F32)
     decay_out = jnp.exp(-rate * (float(BLOCK) - rows_iota(BLOCK)))
     over_block = jnp.exp(-rate * float(BLOCK))
+    flags_copy.wait()
+    for copy in parts:
+        copy.wait()
+    pieces = []
     for b in range(blocks):
-        for copy in parts[b]:
-            copy.wait()
         rows = block_rows(b)
-        pairs_ref[b] = dot_split(k_ref[rows], decay_out * v_ref[rows].astype(F32), 0)
-    flags_copy.wait()
+        pieces.append(dot_split(k_ref[rows], decay_out * v_ref[rows].astype(F32), 0))
     unbroken = 1.0
     carried = jnp.zeros((WIDTH, WIDTH), F32)
     for b in range(blocks):
         keep = 1.0 - flags_smem[0, b].astype(F32)
         unbroken = unbroken * keep
         facts_ref[b + 1 : b + 2] = jnp.full((1, BLOCK), keep, F32)
-        carried = carried * (over_block * keep) + pairs_ref[b]
+        pairs_ref[b] = pieces[b]
+        carried = carried * (over_block * keep) + pieces[b]
     own_ref[:WIDTH] = carried
     own_ref[WIDTH:] = jnp.full((8, WIDTH), unbroken, F32)
     for copy in rest:
@@ -201,12 +197,12 @@
     over_slab = power(facts_ref, float(tokens))
     slabs = all_ref.shape[0]
     state = jnp.zeros((WIDTH, WIDTH), F32)
-    for c in range(slabs // 2):
+    along = jnp.ones((1, WIDTH), F32)
+    for c in reversed(range(slabs // 2)):
         before = c < chip
         factor = all_ref[2 * c, HALF : HALF + 1] * all_ref[2 * c + 1, HALF : HALF + 1]
-        state = jnp.where(
-            before, state * (factor * over_slab * over_slab) + chip_state(all_ref, c), state
-        )
+        state = state + chip_state(all_ref, c) * jnp.where(before, along, 0.0)
+        along = jnp.where(before, along * (factor * over_slab * over_slab), along)
     state = jnp.where(
         core == 1,
         state * (other_ref[WIDTH : WIDTH + 1] * over_slab) + other_ref[:WIDTH],
@@ -226,14 +222,15 @@
 
     def across(b):
         high, low = split(states_ref[b])
-        return dot(q_ref[block_rows(b)], beside(high, low))
+        q = q_ref[block_rows(b)]
+        return dot(beside(q, q), jnp.concatenate([high, low], axis=0))
 
     ahead, behind = across(0), None
     for b in range(blocks + 1):
         coming = across(b + 1) if b + 1 < blocks else None
         if b < blocks:
             rows = block_rows(b)
-            attended = local_ref[rows] + decay_in * halves(ahead)
+            attended = local_ref[rows] + decay_in * ahead
             attended_ref[rows] = attended
             opening = jax.nn.sigmoid(gate_ref[rows].astype(F32))
             grad_norm = cotangent_ref[rows].astype(F32) * opening * gain_ref[...]
@@ -428,7 +425,8 @@
     value_part_ref,
     key_grad_hbm,
     value_grad_hbm,
-    gain_grad_ref,
+    gain_grad_hbm,
+    gain_row,
     key_rows,
     value_rows,
     sems,
@@ -439,39 +437,57 @@
     over_slab = power(facts_ref, float(tokens))
     slabs = all_ref.shape[0]
     state = jnp.zeros((WIDTH, WIDTH), F32)
-    for c in reversed(range(slabs // 2)):
+    along = jnp.ones((1, WIDTH), F32)
+    for c in range(slabs // 2):
         after = c > chip
         factor = unbroken_ref[2 * c : 2 * c + 1] * unbroken_ref[2 * c + 1 : 2 * c + 2]
-        state = jnp.where(
-            after, state * (factor * over_slab * over_slab) + chip_state(all_ref, c), state
-        )
+        state = state + chip_state(all_ref, c) * jnp.where(after, along, 0.0)
+        along = jnp.where(after, along * (factor * over_slab * over_slab), along)
     partner = unbroken_ref[pl.ds(place - core + 1, 1)]
     state = jnp.where(core == 0, state * (partner * over_slab) + other_ref[...], state)
     gain = all_ref[0, HALF : HALF + 1]
     for s in range(1, slabs):
         gain = gain + all_ref[s, HALF : HALF + 1]
-    gain_grad_ref[...] = gain
+    gain_row[...] = gain
+    copies.append(pltpu.make_async_copy(gain_row, gain_grad_hbm, sems.at[2 * (tokens // BLOCK)]))
+    copies[0].start()
     decay_back = jnp.exp(-rate_row(facts_ref) * (float(BLOCK - 1) - rows_iota(BLOCK)))
     over_block = power(facts_ref, float(BLOCK))
     last = tokens // BLOCK - 1
+    sides = [None] * (last + 1)
     for b in reversed(range(last + 1)):
-        rows = block_rows(b)
         if b < last:
             state = state * kept(facts_ref, b + 1)
-        high, low = split(state)
-        both = dot(k_ref[rows], beside(high, low))
-        value_rows[rows] = (value_part_ref[rows] + decay_back * halves(both)).astype(BF16)
-        both = dot(v_ref[rows], jnp.concatenate([high, low], axis=0), 1, 1)
-        key_rows[rows] = (key_part_ref[rows] + decay_back * halves(both)).astype(BF16)
-        for i, (source, target) in enumerate(
-            ((key_rows, key_grad_hbm), (value_rows, value_grad_hbm))
+        sides[b] = split(state)
+        state = state * over_block + pieces_ref[b]
+
+    def products(b):
+        high, low = sides[b]
+        k, v = k_ref[block_rows(b)], v_ref[block_rows(b)]
+        return (
+            dot(beside(k, k), jnp.concatenate([high, low], axis=0)),
+            dot(beside(v, v), beside(high, low), 1, 1),
+        )
+
+    ahead = products(last)
+    for b in reversed(range(last + 1)):
+        coming = products(b - 1) if b > 0 else None
+        rows = block_rows(b)
+        for i, (product, part, source, target) in enumerate(
+            (
+                (ahead[0], value_part_ref, value_rows, value_grad_hbm),
+                (ahead[1], key_part_ref, key_rows, key_grad_hbm),
+            )
         ):
-            copy = pltpu.make_async_copy(
-                source.at[rows], target.at[0, rows], sems.at[2 * b + i]
-            )
-            copy.start()
-            copies.append(copy)
-        state = state * over_block + pieces_ref[b]
+            source[rows] = (part[rows] + decay_back * product).astype(BF16)
+            if b % 2 == 0:
+                done = pl.ds(b * BLOCK, 2 * BLOCK)
+                copy = pltpu.make_async_copy(
+                    source.at[done], target.at[0, done], sems.at[2 * b + i]
+                )
+                copy.start()
+                copies.append(copy)
+        ahead = coming
     for copy in copies:
         copy.wait()
 
@@ -549,7 +565,7 @@
         ins=[SMEM] + [HBM] * 5,
         scratch=[
             pltpu.SMEM((1, blocks), jnp.int32),
-            dma((3 + 2 * blocks,)),
+            dma((5,)),
         ],
     )
     other = lax.ppermute(own, "ctx", partners)
@@ -621,11 +637,12 @@
         ),
         [whole, whole, shape(1, WIDTH)],
         ins=[SMEM],
-        out_specs=[HBM] * 2 + [VMEM],
+        out_specs=[HBM] * 3,
         scratch=[
+            pltpu.VMEM((1, WIDTH), F32),
             pltpu.VMEM((tokens, WIDTH), BF16),
             pltpu.VMEM((tokens, WIDTH), BF16),
-            dma((2 * blocks,)),
+            dma((2 * blocks + 1,)),
         ],
     )
     return (mixed_out, query_grad, key_grad, value_grad, gate_grad, gain_grad)

time: 93.7 us -> 92.7 us (0.989)
  Pallas kernels: 9.82 us -> 8.84 us
    pallas_call x10, Pallas kernels: 9.82 us -> 8.84 us  [call(): pl.pallas_call(kernel, out_shape=outs, in_specs=ins + [VMEM] * (len(array...]
where the time goes in v4:
time: 92.7 us; the launch traced here: 92.3 us
  blocking collectives  39.5 us (43%)
  starting transfers between devices  32.6 us (35%)
  waiting for transfers between devices  10.1 us (11%)
  Pallas kernels  8.84 us (10%)
  between operations  1.38 us (1%)
    all_gather x1, blocking collectives, body(): back_everyone = lax.all_gather(back_half, 'ctx')  16.5 us
    all_gather x1, blocking collectives, body(): everyone = lax.all_gather(half, 'ctx')  16.3 us
    ppermute x1, starting transfers between devices, body(): other = lax.ppermute(own, 'ctx', partners)  16 us
    all_to_all x1, starting transfers between devices, body(): sums = lax.all_to_all(sums, 'dp', 0, 0, tiled=True)  10.7 us
    all_to_all x1, waiting for transfers between devices, body(): sums = lax.all_to_all(sums, 'dp', 0, 0, tiled=True)  9.83 us
    pallas_call x10, Pallas kernels, call(): pl.pallas_call(kernel, out_shape=outs, in_specs=ins + [VMEM] * (len(array...  8.84 us
    all_to_all x1, blocking collectives, body(): sums = lax.all_to_all(sums, 'pipe', 0, 0, tiled=True)  6.65 us
    ppermute x1, starting transfers between devices, body(): back_other = lax.ppermute(back, 'ctx', partners)  5.92 us
  transfers between devices with their start and end apart: 3, of which 2 were waited for; matrix products, arithmetic and copies ran while one was open for 0% of the time, Pallas kernels for 4%

profile of v4, /device:TPU:1, one launch (start us, length us, event | category | flops | bytes accessed | tf_op | source)
XLA Modules:
  0.0 92.3 jit_solution(16203112452555214762)
XLA Ops:
  1.3 1.3 %shard_map.127 = (f32[136,128]{1,0:T(8,128)S(1)}, f32[4,128,128]{2,1,0:T(8,128)S(1)}, f32[8,256]{1,0:T(8,128)S(1)}, bf16[1024,128]{1,0:T(8,128)(2,1)S(1)}, bf16[...) custom-call(f32[1]{0:T(128)S(6)} %copy.14.rate_ref, s32[1,4]{1,0:T(1,128)} %flags_hbm.1, ...), custom_call_target="tpu_custom_call" | custom-call | flops 16777216 | bytes 1913876 | tf_op jit(solution)/shard_map/pallas_call | solution.py:503
  2.6 16.0 %collective-permute-start = (f32[136,128]{1,0:T(8,128)S(1)}, f32[136,128]{1,0:T(8,128)S(1)}, u32[]{:S(2)}, u32[]{:S(2)}) collective-permute-start(f32[136,128]{1,0:T(8,128)S(1)} %get-tuple-element.36.refs_2_), channel_id=1, source_target_pairs={{0,64},{64,0},{128,192},{192,128},{256,320},{320,256},{384,448},{4... | collective-permute-start | bytes 208904 | tf_op jit(solution)/shard_map/ppermute | solution.py:571
  18.7 0.7 shard_map.129.refs_6_
  19.3 0.2 collective-permute-done.refs_3_
  19.6 0.0 copy-start
  19.6 0.0 copy-start.1
  19.6 16.3 %all-gather = f32[1152,128]{1,0:T(8,128)S(1)} all-gather(f32[72,128]{1,0:T(8,128)S(1)} %shard_map.128), channel_id=2, replica_groups=mesh['ctx'=16,'dp'=16,'pipe'=4] {'ctx'}, dimensions={0}, use_global_device_ids=true | all-gather | bytes 626688 | tf_op jit(solution)/shard_map/all_gather | solution.py:579
  35.9 0.0 copy-done
  35.9 0.0 copy-done.1
  35.9 0.7 shard_map.130
  36.6 6.7 %all_to_all.10.parts_ref = f32[4,2,1024]{2,1,0:T(2,128)S(1)} all-to-all(f32[4,2,1024]{2,1,0:T(2,128)S(1)} %get-tuple-element.39), channel_id=1, replica_groups=mesh['ctx'=16,'dp'=16,'pipe'=4] {'pipe'}, dimensions={0} | all-to-all | bytes 65536 | tf_op jit(solution)/shard_map/all_to_all | solution.py:586
  43.2 0.7 shard_map.131
  43.9 10.7 %all-to-all-start.1 = ((f32[16,2,1024]{2,1,0:T(2,128)}), f32[16,2,1024]{2,1,0:T(2,128)S(1)}, u32[]{:S(2)}, u32[]{:S(2)}) async-start(f32[16,2,1024]{2,1,0:T(2,128)} %shard_map.131), calls=%async_computation.1 | async-start | bytes 262144 | tf_op jit(solution)/shard_map/all_to_all | solution.py:588
  54.6 2.1 %shard_map.132.refs_7_ = f32[2,1024,128]{2,1,0:T(8,128)S(1)} custom-call(f32[8,256]{1,0:T(8,128)S(1)} %get-tuple-element.32.refs_1_.facts_ref.refs_0_, bf16[1024,128]{1,0:T(8,128)(2,1)S(1)} %get-tuple-element.34.k_ref.refs_6_, bf16[1024,128]{1,0:T(8,128)(2,1)S(1)} %get-tuple-element.35.v_ref.refs_7_, bf16[1024,128]{1,0:T(8,128)(2,1)S(1)} %bitcast.8, ...), custom_call_target="tpu_custom_call" | custom-call | flops 1073741824 | bytes 2892288 | tf_op jit(solution)/shard_map/pallas_call | solution.py:503
  56.7 9.8 %all-to-all-done.1.refs_1_ = f32[16,2,1024]{2,1,0:T(2,128)S(1)} async-done(((f32[16,2,1024]{2,1,0:T(2,128)}), f32[16,2,1024]{2,1,0:T(2,128)S(1)}, u32[]{:S(2)}, u32[]{:S(2)}) %all-to-all-start.1) | async-done | bytes 131104 | tf_op jit(solution)/shard_map/all_to_all | solution.py:588
  66.5 1.0 %shard_map.133 = (f32[128,128]{1,0:T(8,128)S(1)}, f32[1,128]{1,0:T(1,128)S(1)}, bf16[1024,256]{1,0:T(8,128)(2,1)S(1)}, f32[4,128,128]{2,1,0:T(8,128)S(1)}, bf16[...) custom-call(f32[8,256]{1,0:T(8,128)S(1)} %get-tuple-element.32.refs_1_.facts_ref.refs_0_, ...), custom_call_target="tpu_custom_call" | custom-call | flops 16777216 | bytes 4137984 | tf_op jit(solution)/shard_map/pallas_call | solution.py:503
  67.5 5.9 %collective-permute-start.1 = (f32[128,128]{1,0:T(8,128)S(1)}, f32[128,128]{1,0:T(8,128)S(1)}, u32[]{:S(2)}, u32[]{:S(2)}) collective-permute-start(f32[128,128]{1,0:T(8,128)S(1)} %get-tuple-element.48.refs_2_), channel_id=1, source_target_pairs={{0,64},{64,0},{128,192},{192,128},{256,320},{320,256},{384,448},{4... | collective-permute-start | bytes 196616 | tf_op jit(solution)/shard_map/ppermute | solution.py:608
  73.4 1.1 %shard_map.134 = (bf16[1,1024,128]{2,1,0:T(8,128)(2,1)}, bf16[1,1024,128]{2,1,0:T(8,128)(2,1)}, bf16[1,1024,128]{2,1,0:T(8,128)(2,1)}, f32[1024,128]{1,0:T(8,128)S(1)}, f32[1024,128]{1,0:T(8,128)S(1)}) custom-call(f32[8,256]{1,0:T(8,128)S(1)} %get-tuple-element.32.refs_1_.facts_ref.refs_0_, bf16[1024,128]{1,0:T(8,128)(2,1)S(1)} %get-tuple-element.33.q_ref.refs_5_.refs_3_, ...), custom_call_target="tpu_custom_call" | custom-call | flops 1073741824 | bytes 3940352 | tf_op jit(solution)/shard_map/pallas_call | solution.py:503
  74.5 0.0 collective-permute-done.1.refs_3_
  74.6 16.5 %all-gather.1 = f32[1152,128]{1,0:T(8,128)S(1)} all-gather(f32[72,128]{1,0:T(8,128)S(1)} %shard_map.135), channel_id=3, replica_groups=mesh['ctx'=16,'dp'=16,'pipe'=4] {'ctx'}, dimensions={0}, use_global_device_ids=true | all-gather | bytes 626688 | tf_op jit(solution)/shard_map/all_gather | solution.py:623
  91.1 1.3 %shard_map.136 = (bf16[1,1024,128]{2,1,0:T(8,128)(2,1)}, bf16[1,1024,128]{2,1,0:T(8,128)(2,1)}, f32[1,128]{1,0:T(1,128)}) custom-call(s32[1]{0:T(128)} %bitcast.refs_0_, f32[8,256]{1,0:T(8,128)S(1)} %get-tuple-element.32.refs_1_.facts_ref.refs_0_, f32[16,72,128]{2,1,0:T(8,128)S(1)} %bitcast.5, f32[128,128]{1,0:T(8,128)S(1)} %collective-permute-done.1.refs_3_, ...), custom_call_target="tpu_custom_call" | custom-call | flops 16777216 | bytes 3031556 | tf_op jit(solution)/shard_map/pallas_call | solution.py:503
  (2 shorter events, 0.0 us)
Async XLA Ops:
  2.6 16.9 %collective-permute-start = (f32[136,128]{1,0:T(8,128)S(1)}, f32[136,128]{1,0:T(8,128)S(1)}, u32[]{:S(2)}, u32[]{:S(2)}) collective-permute-start(f32[136,128]{1,0:T(8,128)S(1)} %get-tuple-element.36.refs_2_), channel_id=1, source_target_pairs={{0,64},{64,0},{128,192},{192,128},{256,320},{320,256},{384,448},{4... | collective-permute-start | bytes 208904 | tf_op jit(solution)/shard_map/ppermute | solution.py:571
  19.6 16.3 %copy-start = (bf16[1,1024,128]{2,1,0:T(8,128)(2,1)S(1)}, bf16[1,1024,128]{2,1,0:T(8,128)(2,1)}, u32[]{:S(2)}) copy-start(bf16[1,1024,128]{2,1,0:T(8,128)(2,1)} %param.11) | copy-start | bytes 786436
  19.6 16.3 %copy-start.1 = (bf16[1,1024,128]{2,1,0:T(8,128)(2,1)S(1)}, bf16[1,1024,128]{2,1,0:T(8,128)(2,1)}, u32[]{:S(2)}) copy-start(bf16[1,1024,128]{2,1,0:T(8,128)(2,1)} %param.12) | copy-start | bytes 786436
  43.9 22.6 %all-to-all-start.1 = ((f32[16,2,1024]{2,1,0:T(2,128)}), f32[16,2,1024]{2,1,0:T(2,128)S(1)}, u32[]{:S(2)}, u32[]{:S(2)}) async-start(f32[16,2,1024]{2,1,0:T(2,128)} %shard_map.131), calls=%async_computation.1 | async-start | bytes 262144 | tf_op jit(solution)/shard_map/all_to_all | solution.py:588
  67.5 7.0 %collective-permute-start.1 = (f32[128,128]{1,0:T(8,128)S(1)}, f32[128,128]{1,0:T(8,128)S(1)}, u32[]{:S(2)}, u32[]{:S(2)}) collective-permute-start(f32[128,128]{1,0:T(8,128)S(1)} %get-tuple-element.48.refs_2_), channel_id=1, source_target_pairs={{0,64},{64,0},{128,192},{192,128},{256,320},{320,256},{384,448},{4... | collective-permute-start | bytes 196616 | tf_op jit(solution)/shard_map/ppermute | solution.py:608
